TPU v7x, 256 devices: a whole 4x4x8 slice. The times are simulated.
256 devices in a mesh: orient: 2 (over x_hi), slab: 128 (over y, x_lo, z, core).
Axes of the slice: x: 4 (x_hi: 2, x_lo: 2; x = x_hi * 2 + x_lo), y: 4, z: 8, core: 2. Of those that a mesh axis runs over, the one named last changes fastest.
Arguments:
- propagator: float32 [64, 128, 128, 128], P('orient', 'slab'), may hold values from 0.2 to 2
- field: float32 [128, 128, 128], P('slab'), may hold values from -12 to 12
- orientations: float32 [3, 64], replicated, may hold values from -1 to 1, as said below
- weights: float32 [64], replicated, may hold values from 0.05 to 0.16
Outputs:
- propagated: float32 [64, 128, 128, 128], P('orient', 'slab')
Inputs may be any that keep to these rules, and one draw needn't show every extreme that they name: Each column of orientations is a unit vector.
All inputs are finite; a program needn't handle non-finite values.
Results may differ from a plain program's by a relative error of at most 0.00024.
Values sent between devices are 32-bit elements; how exact they have to be, the bound alone decides.
No kernel may reach another device: no remote copies, remote signals or barrier semaphores. Data moves between devices by JAX's collectives and lax.ppermute only.
A program may use at most 64 MiB of HBM per device.

v0:
```python
import math

import jax
import jax.numpy as jnp
from jax import lax
from jax.sharding import PartitionSpec as P

LMAX = 10


HALF_STEP = 0.1
BOX_LENGTH = 12.8
DECAY_RATE = 0.01
HIGHEST = lax.Precision.HIGHEST
HIGH = lax.Precision.HIGH
AXES = ("orient", "slab")


def packed_tables(length):
    half = length // 2
    positions = jnp.arange(length, dtype=jnp.int32)
    orders = jnp.arange(half, dtype=jnp.int32)
    angles = (positions[:, None] * orders[None, :] % length).astype(jnp.float32) * (2.0 * math.pi / length)
    nyquist = jnp.where(positions % 2 == 0, 1.0, -1.0).astype(jnp.float32)
    sines = jnp.where(orders[None, :] == 0, nyquist[:, None], jnp.sin(angles))
    forward = jnp.concatenate([jnp.cos(angles), sines], axis=1)
    scale = jnp.where(jnp.arange(length) % half == 0, 1.0, 2.0).astype(jnp.float32) / length
    return forward, forward * scale[None, :]


def phase_tables(components, length):
    step = HALF_STEP * 2.0 * math.pi / BOX_LENGTH
    angles = components[:, None] * (jnp.arange(length // 2, dtype=jnp.float32) * step)[None, :]
    return jnp.cos(angles), jnp.sin(angles)


def shift_matrices(components, length):
    half = length // 2
    forward, inverse = packed_tables(length)
    cosines, sines = phase_tables(components, length)
    left_cos, left_sin = inverse[None, :, :half], inverse[None, :, half:]
    rotated = jnp.concatenate(
        [
            left_cos * cosines[:, None, :] + left_sin * sines[:, None, :],
            left_sin * cosines[:, None, :] - left_cos * sines[:, None, :],
        ],
        axis=2,
    )
    return jnp.einsum("oik,jk->oij", rotated, forward, precision=HIGH)


def mixing_matrix(orientations, weights):
    cosines = jnp.dot(orientations.T, orientations, precision=HIGHEST)
    previous = jnp.ones_like(cosines)
    current = cosines
    combined = previous * (1.0 / (4.0 * math.pi))
    for degree in range(1, LMAX + 1):
        if degree > 1:
            previous, current = (
                current,
                ((2 * degree - 1) * cosines * current - (degree - 1) * previous) / degree,
            )
        combined = (
            combined
            + math.exp(-DECAY_RATE * degree * (degree + 1))
            * (2 * degree + 1)
            / (4.0 * math.pi)
            * current
        )
    return combined * weights[None, :]


def local(propagator, field, orientations, weights):
    own, depth, rows, cols = propagator.shape
    groups = lax.axis_size("orient")
    slabs = lax.axis_size("slab")
    start = lax.axis_index("orient") * own
    directions = lax.dynamic_slice_in_dim(orientations, start, own, 1)
    damping = jnp.exp(-0.5 * HALF_STEP * field[0])
    damped = propagator[:, 0] * damping[None]
    shift_x = shift_matrices(directions[0], cols)
    shift_y = shift_matrices(directions[1], rows)
    moved = jnp.einsum("oyx,oix->oyi", damped, shift_x, precision=HIGH)
    moved = jnp.einsum("ojy,oyi->oji", shift_y, moved, precision=HIGH)
    width = cols // groups
    sent = moved.reshape(own, slabs, groups, width).transpose(2, 1, 0, 3).reshape(groups * slabs, own * width)
    lines = lax.all_to_all(sent, AXES, 0, 0, tiled=True)
    total_z = depth * slabs
    lines = lines.reshape(groups, total_z, own, width)
    forward, inverse = packed_tables(total_z)
    half = total_z // 2
    spectrum = jnp.einsum("hzow,zk->khow", lines, forward, precision=HIGH)
    cosines, sines = phase_tables(orientations[2], total_z)
    cosines = cosines.T.reshape(half, groups, own, 1)
    sines = sines.T.reshape(half, groups, own, 1)
    first, second = spectrum[:half], spectrum[half:]
    spectrum = jnp.concatenate(
        [first * cosines - second * sines, first * sines + second * cosines], axis=0
    )
    advected = jnp.einsum("khow,zk->hozw", spectrum, inverse, precision=HIGH)
    matrix = mixing_matrix(orientations, weights)
    mixed = jnp.dot(matrix, advected.reshape(groups * own, total_z * width), precision=HIGH)
    back = mixed.reshape(groups, own, total_z, width).transpose(0, 2, 1, 3).reshape(groups * slabs, own * width)
    final = lax.all_to_all(back, AXES, 0, 0, tiled=True)
    final = final.reshape(groups, slabs, own, width).transpose(2, 1, 0, 3).reshape(own, 1, rows, cols)
    return final * damping[None, None]


def solution(mesh):
    in_specs = (P("orient", "slab", None, None), P("slab", None, None), P(), P())
    out_specs = P("orient", "slab", None, None)
    return jax.shard_map(local, mesh=mesh, in_specs=in_specs, out_specs=out_specs, check_vma=False)
```

profile of v0, /device:TPU:1, one launch (start us, length us, event | category | flops | bytes accessed | tf_op | source)
XLA Modules:
  0.0 202.1 jit_solution(5540022205641191878)
XLA Ops:
  0.0 0.8 constant_dynamic-slice_fusion
  0.8 0.3 sine_select_fusion
  1.1 0.1 broadcast_multiply_fusion
  1.2 0.1 fusion.30
  1.3 0.9 exponential_bitcast_fusion
  2.1 0.2 multiply_cosine_fusion.1
  2.3 1.2 multiply_add_fusion.1
  3.5 1.3 fusion.4
  4.8 0.0 copy-start
  4.9 1.3 fusion
  6.2 0.3 copy-done
  6.4 2.3 %fusion.10 = f32[32,128,128]{1,2,0:T(8,128)S(1)} fusion(f32[32,128,128]{2,1,0:T(8,128)S(1)} %fusion.4, f32[32,1,128,128]{3,2,1,0:T(8,128)S(1)} %copy-done, f32[128,128]{1,0:T(8,128)S(1)} %exponential_bitcast_fusion), kind=kOutput, calls=%fused_computation.13 | convolution fusion | flops 403177472 | bytes 6356992 | tf_op jit(solution)/shard_map/oyx,oix->oyi/dot_general | solution.py:83
  8.8 2.3 %fusion.31 = f32[32,128,128]{1,2,0:T(8,128)S(1)} fusion(f32[32,128,128]{2,1,0:T(8,128)S(1)} %fusion, f32[32,128,128]{1,2,0:T(8,128)S(1)} %fusion.10), kind=kOutput, calls=%fused_computation.64 | convolution fusion | flops 402653184 | bytes 6291456 | tf_op jit(solution)/shard_map/ojy,oyi->oji/dot_general | solution.py:84
  11.1 1.7 copy.33
  12.8 2.7 %all_to_all.12 = f32[256,1,2048]{0,2,1:T(8,128)} reshape(f32[2,128,32,64]{1,0,3,2:T(2,128)S(1)} %bitcast.68) | data formatting | bytes 4194304 | tf_op jit(solution)/shard_map/all_to_all | solution.py:87
  15.5 6.1 %copy.15 = f32[256,1,2048]{2,1,0:T(1,128)} copy(f32[256,1,2048]{0,2,1:T(8,128)} %all_to_all.12) | data formatting | bytes 4194304 | tf_op jit(solution)/shard_map/all_to_all | solution.py:87
  21.6 0.0 copy-start.1
  21.6 0.0 copy-start.2
  21.6 16.7 %all-to-all-start = ((f32[256,1,2048]{2,1,0:T(1,128)}), f32[256,1,2048]{2,1,0:T(1,128)}, u32[]{:S(2)}, u32[]{:S(2)}) async-start(f32[256,1,2048]{2,1,0:T(1,128)} %copy.15), calls=%async_computation | async-start | bytes 4194304 | tf_op jit(solution)/shard_map/all_to_all | solution.py:87
  38.2 0.0 copy-done.1
  38.3 0.1 mul.563
  38.4 0.0 copy-done.2
  38.4 0.3 add_multiply_fusion
  38.7 0.2 multiply_cosine_fusion
  38.9 51.7 %all-to-all-done = f32[256,1,2048]{2,1,0:T(1,128)} async-done(((f32[256,1,2048]{2,1,0:T(1,128)}), f32[256,1,2048]{2,1,0:T(1,128)}, u32[]{:S(2)}, u32[]{:S(2)}) %all-to-all-start) | async-done | bytes 2097184 | tf_op jit(solution)/shard_map/all_to_all | solution.py:87
  90.5 6.6 %reduce = f32[256,2048]{1,0:T(8,128)S(1)} reduce(f32[256,1,2048]{2,1,0:T(1,128)} %all-to-all-done, f32[]{:T(128)} %constant.174), dimensions={1}, to_apply=%all_to_all.13.reduce_sub_computation | reduce | bytes 4194308 | tf_op jit(solution)/shard_map/all_to_all | solution.py:87
  97.1 3.0 %reshape.232 = f32[2,128,32,64]{3,2,1,0:T(8,128)} reshape(f32[256,2048]{1,0:T(8,128)S(1)} %reduce) | data formatting | bytes 4194304 | tf_op jit(solution)/shard_map/reshape | solution.py:89
  100.1 3.8 %copy.17 = f32[2,128,32,64]{1,3,2,0:T(8,128)S(1)} copy(f32[2,128,32,64]{3,2,1,0:T(8,128)} %reshape.232) | data formatting | bytes 4194304 | tf_op jit(solution)/shard_map/reshape | solution.py:89
  103.9 1.0 fusion.32
  104.9 0.8 multiply_subtract_fusion
  105.7 0.6 pad_maximum_fusion
  106.3 1.0 fusion.33
  107.4 2.7 %copy.18 = f32[2,32,128,64]{3,2,1,0:T(8,128)} copy(f32[2,32,128,64]{2,3,1,0:T(8,128)S(1)} %bitcast.67) | data formatting | bytes 4194304 | tf_op jit(solution)/shard_map/khow,zk->hozw/transpose | solution.py:100
  110.1 3.5 %reshape.222 = f32[64,8192]{1,0:T(8,128)S(1)} reshape(f32[2,32,128,64]{3,2,1,0:T(8,128)} %copy.18) | data formatting | bytes 4194304 | tf_op jit(solution)/shard_map/reshape | solution.py:102
  113.6 3.0 %dot_general.39 = f32[128,64,64]{1,0,2:T(8,128)} reshape(f32[8192,64]{0,1:T(8,128)S(1)} %bitcast.63) | data formatting | bytes 4194304 | tf_op jit(solution)/shard_map/dot_general | solution.py:102
  116.6 3.5 %copy.19 = f32[128,64,64]{0,2,1:T(8,128)S(1)} copy(f32[128,64,64]{1,0,2:T(8,128)} %dot_general.39) | data formatting | bytes 4194304 | tf_op jit(solution)/shard_map/dot_general | solution.py:102
  120.2 2.3 %fusion.11 = f32[2,128,32,64]{1,2,3,0:T(8,128)} fusion(f32[2,32,64,1]{2,1,3,0:T(8,128)S(1)} %bitcast.70, f32[128,64,64]{0,2,1:T(8,128)S(1)} %copy.19), kind=kOutput, calls=%fused_computation.21 | convolution fusion | flops 201326592 | bytes 4210688 | tf_op jit(solution)/shard_map/dot_general | solution.py:102
  122.4 5.6 %copy.30 = f32[2,128,32,64]{3,2,1,0:T(8,128)} copy(f32[2,128,32,64]{1,2,3,0:T(8,128)} %fusion.11) | data formatting | bytes 4194304 | tf_op jit(solution)/shard_map/all_to_all | solution.py:104
  128.0 5.6 %reshape.233 = f32[256,1,2048]{2,1,0:T(1,128)} reshape(f32[2,128,32,64]{3,2,1,0:T(8,128)} %copy.30) | data formatting | bytes 4194304 | tf_op jit(solution)/shard_map/all_to_all | solution.py:104
  133.6 6.6 %all-to-all-start.1 = ((f32[256,1,2048]{2,1,0:T(1,128)}), f32[256,1,2048]{2,1,0:T(1,128)S(1)}, u32[]{:S(2)}, u32[]{:S(2)}) async-start(f32[256,1,2048]{2,1,0:T(1,128)} %reshape.233), calls=%async_computation.1 | async-start | bytes 4194304 | tf_op jit(solution)/shard_map/all_to_all | solution.py:104
  140.2 0.1 copy.24
  140.3 53.1 %all-to-all-done.1 = f32[256,1,2048]{2,1,0:T(1,128)S(1)} async-done(((f32[256,1,2048]{2,1,0:T(1,128)}), f32[256,1,2048]{2,1,0:T(1,128)S(1)}, u32[]{:S(2)}, u32[]{:S(2)}) %all-to-all-start.1) | async-done | bytes 2097184 | tf_op jit(solution)/shard_map/all_to_all | solution.py:104
  193.4 4.0 %copy.22 = f32[256,1,2048]{0,2,1:T(8,128)} copy(f32[256,1,2048]{2,1,0:T(1,128)S(1)} %all-to-all-done.1) | data formatting | bytes 4194304 | tf_op jit(solution)/shard_map/all_to_all | solution.py:104
  197.3 2.3 %reshape.223 = f32[2,128,32,64]{1,0,3,2:T(2,128)S(1)} reshape(f32[256,1,2048]{0,2,1:T(8,128)} %copy.22) | data formatting | bytes 4194304 | tf_op jit(solution)/shard_map/reshape | solution.py:105
  199.6 0.3 copy.23
  199.9 0.3 bitcast_multiply_fusion
  200.3 1.8 copy.25
  (6 shorter events, 0.0 us)
Async XLA Ops:
  4.8 1.6 copy-start
  21.6 16.7 %copy-start.1 = (f32[3,64]{1,0:T(4,128)S(1)}, f32[3,64]{1,0:T(4,128)}, u32[]{:S(2)}) copy-start(f32[3,64]{1,0:T(4,128)} %param.6) | copy-start | bytes 2308
  21.6 16.8 %copy-start.2 = (f32[64]{0:T(128)S(1)}, f32[64]{0:T(128)}, u32[]{:S(2)}) copy-start(f32[64]{0:T(128)} %param.7) | copy-start | bytes 772
  21.6 69.0 %all-to-all-start = ((f32[256,1,2048]{2,1,0:T(1,128)}), f32[256,1,2048]{2,1,0:T(1,128)}, u32[]{:S(2)}, u32[]{:S(2)}) async-start(f32[256,1,2048]{2,1,0:T(1,128)} %copy.15), calls=%async_computation | async-start | bytes 4194304 | tf_op jit(solution)/shard_map/all_to_all | solution.py:87
  133.6 59.8 %all-to-all-start.1 = ((f32[256,1,2048]{2,1,0:T(1,128)}), f32[256,1,2048]{2,1,0:T(1,128)S(1)}, u32[]{:S(2)}, u32[]{:S(2)}) async-start(f32[256,1,2048]{2,1,0:T(1,128)} %reshape.233), calls=%async_computation.1 | async-start | bytes 4194304 | tf_op jit(solution)/shard_map/all_to_all | solution.py:104
where the time goes:
time: 203 us; the launch traced here: 202 us
  waiting for transfers between devices  105 us (52%)
  local copies, waits for them, and re-layouts  50.8 us (25%)
  starting transfers between devices  23.3 us (11%)
  matrix products  11.8 us (6%)
  other arithmetic  11.2 us (6%)
    all_to_all x1, waiting for transfers between devices, local(): final = lax.all_to_all(back, AXES, 0, 0, tiled=True)  53.1 us
    all_to_all x1, waiting for transfers between devices, local(): lines = lax.all_to_all(sent, AXES, 0, 0, tiled=True)  51.7 us
    all_to_all x1, starting transfers between devices, local(): lines = lax.all_to_all(sent, AXES, 0, 0, tiled=True)  16.7 us
    all_to_all x3, local copies, waits for them, and re-layouts, local(): final = lax.all_to_all(back, AXES, 0, 0, tiled=True)  15.1 us
    all_to_all x2, local copies, waits for them, and re-layouts, local(): lines = lax.all_to_all(sent, AXES, 0, 0, tiled=True)  8.77 us
    reshape x2, local copies, waits for them, and re-layouts, local(): lines = lines.reshape(groups, total_z, own, width)  6.79 us
    all_to_all x1, starting transfers between devices, local(): final = lax.all_to_all(back, AXES, 0, 0, tiled=True)  6.63 us
    all_to_all x1, other arithmetic, local(): lines = lax.all_to_all(sent, AXES, 0, 0, tiled=True)  6.58 us
  transfers between devices with their start and end apart: 2, of which 2 were waited for; matrix products, arithmetic and copies ran while one was open for 0% of the time, Pallas kernels for 0%

commit v1 on v0

v1 whole, which is shorter than its diff:
```python
import functools
import math

import jax
import jax.numpy as jnp
import numpy as np
from jax import lax
from jax.experimental import pallas as pl
from jax.experimental.pallas import tpu as pltpu
from jax.sharding import PartitionSpec as P

LMAX = 10


HALF_STEP = 0.1
BOX_LENGTH = 12.8
DECAY_RATE = 0.01
HIGHEST = lax.Precision.HIGHEST
AXES = ("orient", "slab")
INTERPRET = False


def packed_tables(length):
    half = length // 2
    positions = np.arange(length)
    orders = np.arange(half)
    angles = (positions[:, None] * orders[None, :] % length) * (2.0 * math.pi / length)
    nyquist = np.where(positions % 2 == 0, 1.0, -1.0)
    sines = np.where(orders[None, :] == 0, nyquist[:, None], np.sin(angles))
    forward = np.concatenate([np.cos(angles), sines], axis=1)
    scale = np.where(np.arange(length) % half == 0, 1.0, 2.0) / length
    return forward.astype(np.float32), (forward * scale[None, :]).astype(np.float32)


def phase_tables(components, length):
    step = HALF_STEP * 2.0 * math.pi / BOX_LENGTH
    angles = components[:, None] * (jnp.arange(length // 2, dtype=jnp.float32) * step)[None, :]
    return jnp.cos(angles), jnp.sin(angles)


def shift_kernels(components, length):
    half = length // 2
    _, inverse = packed_tables(length)
    cosines, sines = phase_tables(components, length)
    sines = jnp.where(jnp.arange(half)[None, :] == 0, 1.0, sines)
    return jnp.dot(jnp.concatenate([cosines, sines], axis=1), jnp.asarray(inverse.T), precision=HIGHEST)


def mixing_matrix(orientations, weights):
    cosines = jnp.dot(orientations.T, orientations, precision=HIGHEST)
    previous = jnp.ones_like(cosines)
    current = cosines
    combined = previous * (1.0 / (4.0 * math.pi))
    for degree in range(1, LMAX + 1):
        if degree > 1:
            previous, current = (
                current,
                ((2 * degree - 1) * cosines * current - (degree - 1) * previous) / degree,
            )
        combined = (
            combined
            + math.exp(-DECAY_RATE * degree * (degree + 1))
            * (2 * degree + 1)
            / (4.0 * math.pi)
            * current
        )
    return combined * weights[None, :]


def halves(values):
    high = values.astype(jnp.bfloat16)
    return high, (values - high.astype(jnp.float32)).astype(jnp.bfloat16)


def wide_table(values):
    high = values.astype(jnp.bfloat16)
    low = (values - high.astype(np.float32)).astype(jnp.bfloat16)
    return np.concatenate([high, high, low], axis=1)


def wide_left(values):
    high, low = halves(values)
    return jnp.concatenate([high, high, low], axis=1)


def wide_right(values):
    high, low = halves(values)
    return jnp.concatenate([high, low, high], axis=0)


def product(left, right):
    return jnp.dot(left, right, preferred_element_type=jnp.float32)


def swap(values):
    return pltpu.roll(values, values.shape[1] // 2, 1)


def low_lanes(shape):
    return lax.broadcasted_iota(jnp.int32, shape, 1) < shape[1] // 2


def circulant(row):
    length = row.shape[1]
    return pltpu.roll(jnp.broadcast_to(row, (length, length)), 0, 1, stride=1, stride_axis=0)


def plane_kernel(propagator_ref, field_ref, kernel_x_ref, kernel_y_ref, out_ref, damping_ref):
    row = pl.program_id(0)
    count = pl.num_programs(0)

    @pl.when(row == 0)
    def _():
        damping_ref[...] = jnp.exp(-0.5 * HALF_STEP * field_ref[...])

    moved = []
    for part in range(2):
        own = part * count + row
        damped = propagator_ref[part, 0] * damping_ref[...]
        shift_x = circulant(kernel_x_ref[pl.ds(own, 1), :])
        shift_y = circulant(kernel_y_ref[pl.ds(own, 1), :])
        along_x = product(wide_left(damped), wide_right(shift_x))
        moved.append(product(wide_left(shift_y), wide_right(along_x)))
    first, second = moved
    low = low_lanes(first.shape)
    rows = pl.ds(row, first.shape[0], stride=count)
    out_ref[0, rows, :] = jnp.where(low, first, swap(second))
    out_ref[1, rows, :] = jnp.where(low, swap(first), second)


def line_kernel(depth, lines_ref, forward_ref, inverse_ref, cos_ref, sin_ref, mixing_ref, out_ref, advected_ref):
    count = lines_ref.shape[1] // depth
    half = depth // 2
    lanes = lines_ref.shape[2]
    pairs = count // 2

    def shift(item, carry):
        group = item // pairs
        row = 2 * (item % pairs)
        taken = [lines_ref[group, pl.ds(row + n, depth, stride=count), :] for n in range(2)]
        spectrum = product(forward_ref[...], wide_right(jnp.concatenate(taken, axis=1)))
        cosines = jnp.concatenate([cos_ref[group, row + n] for n in range(2)], axis=1)
        sines = jnp.concatenate([sin_ref[group, row + n] for n in range(2)], axis=1)
        real, imaginary = spectrum[:half], spectrum[half:]
        turned = jnp.concatenate(
            [real * cosines - imaginary * sines, real * sines + imaginary * cosines], axis=0
        )
        advected = product(inverse_ref[...], wide_right(turned))
        for n in range(2):
            rows = pl.ds(group * count + row + n, depth, stride=2 * count)
            advected_ref[rows, :] = advected[:, n * lanes : (n + 1) * lanes]
        return carry

    lax.fori_loop(0, 2 * pairs, shift, 0)
    both = 2 * count
    mixing = wide_left(mixing_ref[...])
    low = low_lanes((both, lanes))

    def mix(step, carry):
        stacked = []
        for n in range(2):
            base = (4 * step + 2 * n) * both
            first = advected_ref[pl.ds(base, both), :]
            second = advected_ref[pl.ds(base + both, both), :]
            stacked.append(
                jnp.concatenate(
                    [jnp.where(low, first, swap(second)), jnp.where(low, swap(first), second)], axis=0
                )
            )
        mixed = product(mixing, wide_right(jnp.concatenate(stacked, axis=1)))
        for n in range(2):
            place = mixed[:, n * lanes : (n + 1) * lanes]
            first, second = place[:both], place[both:]
            for m, values in enumerate(
                (jnp.where(low, first, swap(second)), jnp.where(low, swap(first), second))
            ):
                target = pl.ds((4 * step + 2 * n + m) * count, count)
                out_ref[0, target, :] = values[:count]
                out_ref[1, target, :] = values[count:]
        return carry

    lax.fori_loop(0, depth // 4, mix, 0)


def close_kernel(mixed_ref, field_ref, out_ref, damping_ref):
    row = pl.program_id(0)
    count = pl.num_programs(0)

    @pl.when(row == 0)
    def _():
        damping_ref[...] = jnp.exp(-0.5 * HALF_STEP * field_ref[...])

    depth = field_ref.shape[0]
    first = mixed_ref[0, pl.ds(row, depth, stride=count), :]
    second = mixed_ref[1, pl.ds(row, depth, stride=count), :]
    low = low_lanes(first.shape)
    damping = damping_ref[...]
    out_ref[0, 0] = jnp.where(low, first, swap(second)) * damping
    out_ref[1, 0] = jnp.where(low, swap(first), second) * damping


def whole(shape):
    return pl.BlockSpec(shape, lambda row: (0,) * len(shape))


def local(propagator, field, orientations, weights):
    own, depth, rows, cols = propagator.shape
    groups = lax.axis_size("orient")
    slabs = lax.axis_size("slab")
    total_z = depth * slabs
    count = own // 2
    half = total_z // 2
    start = lax.axis_index("orient") * own
    directions = lax.dynamic_slice_in_dim(orientations, start, own, 1)
    kernel_x = shift_kernels(directions[0], cols)
    kernel_y = shift_kernels(-directions[1], rows)
    plane = field[0]
    message = (groups, slabs * count, cols)
    sent = pl.pallas_call(
        plane_kernel,
        grid=(count,),
        in_specs=[
            pl.BlockSpec((2, 1, rows, cols), lambda row: (0, row, 0, 0)),
            whole((rows, cols)),
            whole((own, cols)),
            whole((own, rows)),
        ],
        out_specs=whole(message),
        out_shape=jax.ShapeDtypeStruct(message, jnp.float32),
        scratch_shapes=[pltpu.VMEM((rows, cols), jnp.float32)],
        interpret=INTERPRET,
        name="plane",
    )(propagator.reshape(2, count, rows, cols), plane, kernel_x, kernel_y)

    lines = lax.all_to_all(sent.reshape(groups * slabs, count, cols), AXES, 0, 0, tiled=True)

    forward, inverse = packed_tables(total_z)
    cosines, sines = phase_tables(orientations[2], total_z)

    def by_lane(table):
        table = table.reshape(groups, 2, count, half).transpose(0, 2, 3, 1)
        return jnp.repeat(table, cols // 2, axis=3)

    matrix = mixing_matrix(orientations, weights)
    matrix = matrix.reshape(groups, 2, count, groups, 2, count).transpose(1, 0, 2, 4, 3, 5)
    matrix = matrix.reshape(2 * own, 2 * own)
    back = pl.pallas_call(
        functools.partial(line_kernel, total_z),
        out_shape=jax.ShapeDtypeStruct(message, jnp.float32),
        scratch_shapes=[pltpu.VMEM((total_z * groups * count, cols), jnp.float32)],
        interpret=INTERPRET,
        name="line",
    )(
        lines.reshape(message),
        wide_table(forward.T),
        wide_table(inverse),
        by_lane(cosines),
        by_lane(sines),
        matrix,
    )
    mixed = lax.all_to_all(back.reshape(groups * slabs, count, cols), AXES, 0, 0, tiled=True)
    result = pl.pallas_call(
        close_kernel,
        grid=(count,),
        in_specs=[whole(message), whole((rows, cols))],
        out_specs=pl.BlockSpec((2, 1, rows, cols), lambda row: (0, row, 0, 0)),
        out_shape=jax.ShapeDtypeStruct((2, count, rows, cols), jnp.float32),
        scratch_shapes=[pltpu.VMEM((rows, cols), jnp.float32)],
        interpret=INTERPRET,
        name="close",
    )(mixed.reshape(message), plane)
    return result.reshape(own, 1, rows, cols)


def solution(mesh):
    in_specs = (P("orient", "slab", None, None), P("slab", None, None), P(), P())
    out_specs = P("orient", "slab", None, None)
    return jax.shard_map(local, mesh=mesh, in_specs=in_specs, out_specs=out_specs, check_vma=False)
```

time: 203 us -> 182 us (0.90)
  waiting for transfers between devices: 105 us -> 34.5 us
  blocking collectives: 0 us -> 59.9 us
  Pallas kernels: 0 us -> 44.4 us
  local copies, waits for them, and re-layouts: 50.8 us -> 16.8 us
  starting transfers between devices: 23.3 us -> 15.6 us
  other arithmetic: 11.2 us -> 3.7 us
  matrix products: 11.8 us -> 5.63 us
    all_to_all x2 -> x1, waiting for transfers between devices: 105 us -> 34.5 us  [local(): lax.all_to_all(sent.reshape(groups * slabs, count, cols), AXES, 0, 0, til...]
    all_to_all x0 -> x1, blocking collectives: none -> 59.9 us  [local(): lax.all_to_all(back.reshape(groups * slabs, count, cols), AXES, 0, 0, til...]
    pallas_call x0 -> x3, Pallas kernels: none -> 44.4 us  [the longest x1 21.4 us: local(): pl.pallas_call(functools.partial(line_kernel, total_z), out_shape=jax.Sha...]
    all_to_all x5 -> x0, local copies, waits for them, and re-layouts: 23.9 us -> none  [the longest x3 15.1 us: local(): final = lax.all_to_all(back, AXES, 0, 0, tiled=True)]
    all_to_all x2 -> x1, starting transfers between devices: 23.3 us -> 15.6 us  [local(): lax.all_to_all(sent.reshape(groups * slabs, count, cols), AXES, 0, 0, til...]
    broadcast_in_dim x0 -> x2, local copies, waits for them, and re-layouts: none -> 6.83 us  [by_lane(): return jnp.repeat(table, cols // 2, axis=3)]
    reshape x5, local copies, waits for them, and re-layouts: 14.3 us -> 7.64 us  [the longest x2 6.66 us: by_lane(): return jnp.repeat(table, cols // 2, axis=3)]
    all_to_all x1 -> x0, other arithmetic: 6.58 us -> none  [local(): lines = lax.all_to_all(sent, AXES, 0, 0, tiled=True)]
  transfers between devices with their start and end apart: 2 -> 1, of which waited for: 2 -> 1; matrix products, arithmetic and copies ran while one was open for 0% -> 10% of each run, Pallas kernels for 0% -> 0%
where the time goes in v1:
time: 182 us; the launch traced here: 181 us
  blocking collectives  59.9 us (33%)
  Pallas kernels  44.4 us (24%)
  waiting for transfers between devices  34.5 us (19%)
  local copies, waits for them, and re-layouts  16.8 us (9%)
  starting transfers between devices  15.6 us (9%)
  matrix products  5.63 us (3%)
  other arithmetic  3.7 us (2%)
    all_to_all x1, blocking collectives, local(): lax.all_to_all(back.reshape(groups * slabs, count, cols), AXES, 0, 0, til...  59.9 us
    all_to_all x1, waiting for transfers between devices, local(): lax.all_to_all(sent.reshape(groups * slabs, count, cols), AXES, 0, 0, til...  34.5 us
    pallas_call x1, Pallas kernels, local(): pl.pallas_call(functools.partial(line_kernel, total_z), out_shape=jax.Sha...  21.4 us
    all_to_all x1, starting transfers between devices, local(): lax.all_to_all(sent.reshape(groups * slabs, count, cols), AXES, 0, 0, til...  15.6 us
    pallas_call x1, Pallas kernels, local(): pl.pallas_call(plane_kernel, grid=(count,), in_specs=[pl.BlockSpec((2, 1,...  14.9 us
    pallas_call x1, Pallas kernels, local(): pl.pallas_call(close_kernel, grid=(count,), in_specs=[whole(message), who...  8.12 us
    broadcast_in_dim x2, local copies, waits for them, and re-layouts, by_lane(): return jnp.repeat(table, cols // 2, axis=3)  6.83 us
    reshape x2, local copies, waits for them, and re-layouts, by_lane(): return jnp.repeat(table, cols // 2, axis=3)  6.66 us
  transfers between devices with their start and end apart: 1, of which 1 were waited for; matrix products, arithmetic and copies ran while one was open for 10% of the time, Pallas kernels for 0%

profile of v1, /device:TPU:1, one launch (start us, length us, event | category | flops | bytes accessed | tf_op | source)
XLA Modules:
  0.0 180.7 jit_solution(18169820379263464389)
XLA Ops:
  0.0 0.8 constant_dynamic-slice_fusion
  0.8 1.0 fusion.6
  1.8 1.0 fusion.3
  2.9 1.6 convolution_add_fusion.kernel_y_ref
  4.5 1.6 convolution_add_fusion.1.kernel_x_ref
  6.1 14.9 %plane.1 = f32[2,2048,128]{2,1,0:T(8,128)} custom-call(f32[2,16,128,128]{3,2,1,0:T(8,128)} %bitcast.27, f32[128,128]{1,0:T(8,128)} %bitcast.29, f32[32,128]{1,0:T(8,128)} %convolution_add_fusion.1.kernel_x_ref, f32[32,128]{1,0:T(8,128)} %convolution_add_fusion.kernel_y_ref), custom_call_target="tpu_custom_call" | custom-call | tf_op jit(solution)/shard_map/plane/pallas_call | solution.py:219
  21.0 0.0 copy-start.1
  21.0 0.0 copy-start.2
  21.0 15.6 %all-to-all-start = ((f32[256,16,128]{2,1,0:T(8,128)}), f32[256,16,128]{2,1,0:T(8,128)S(1)}, u32[]{:S(2)}, u32[]{:S(2)}) async-start(f32[256,16,128]{2,1,0:T(8,128)} %bitcast.25), calls=%async_computation | async-start | bytes 4194304 | tf_op jit(solution)/shard_map/all_to_all | solution.py:235
  36.7 0.0 copy-done.1
  36.7 0.1 mul.251
  36.8 0.1 copy.9
  36.9 0.0 copy-done.2
  36.9 0.3 add_multiply_fusion
  37.2 0.2 reshape.75
  37.4 0.1 copy.13
  37.4 0.8 reshape.76.mixing_ref
  38.2 3.7 %multiply_sine_fusion = (f32[2,16,64,2]{3,2,1,0:T(8,128)S(1)}, f32[2,16,64,2]{3,2,1,0:T(8,128)S(1)}) fusion(f32[64]{0:T(128)S(1)} %iota_multiply_fusion, f32[2,16,2]{2,1,0:T(8,128)S(1)} %copy.9), kind=kLoop, calls=%fused_computation | loop fusion | flops 4096 | bytes 33280 | tf_op jit(solution)/shard_map/sin | solution.py:38
  41.9 3.4 %broadcast_in_dim.35 = f32[2,16,64,2,64]{4,3,2,1,0:T(2,128)} broadcast(f32[2,16,64,2]{3,2,1,0:T(8,128)S(1)} %get-tuple-element.5), dimensions={0,1,2,3} | broadcast | bytes 1064960 | tf_op jit(solution)/shard_map/broadcast_in_dim | solution.py:242
  45.3 3.3 %reshape.74.sin_ref = f32[2,16,64,128]{3,2,1,0:T(8,128)} reshape(f32[2,16,64,2,64]{4,3,2,1,0:T(2,128)} %broadcast_in_dim.35) | data formatting | bytes 2097152 | tf_op jit(solution)/shard_map/reshape | solution.py:242
  48.7 3.4 %broadcast_in_dim.34 = f32[2,16,64,2,64]{4,3,2,1,0:T(2,128)} broadcast(f32[2,16,64,2]{3,2,1,0:T(8,128)S(1)} %get-tuple-element.6), dimensions={0,1,2,3} | broadcast | bytes 1064960 | tf_op jit(solution)/shard_map/broadcast_in_dim | solution.py:242
  52.1 3.3 %reshape.73.cos_ref = f32[2,16,64,128]{3,2,1,0:T(8,128)} reshape(f32[2,16,64,2,64]{4,3,2,1,0:T(2,128)} %broadcast_in_dim.34) | data formatting | bytes 2097152 | tf_op jit(solution)/shard_map/reshape | solution.py:242
  55.4 34.5 %all-to-all-done = f32[256,16,128]{2,1,0:T(8,128)S(1)} async-done(((f32[256,16,128]{2,1,0:T(8,128)}), f32[256,16,128]{2,1,0:T(8,128)S(1)}, u32[]{:S(2)}, u32[]{:S(2)}) %all-to-all-start) | async-done | bytes 2097184 | tf_op jit(solution)/shard_map/all_to_all | solution.py:235
  89.9 0.0 copy-start
  89.9 1.3 copy-done
  91.2 21.4 %line.1 = f32[2,2048,128]{2,1,0:T(8,128)} custom-call(f32[2,2048,128]{2,1,0:T(8,128)} %bitcast.23, bf16[128,384]{1,0:T(8,128)(2,1)} %constant.113.clone.forward_ref, bf16[128,384]{1,0:T(8,128)(2,1)} %constant.114.clone.inverse_ref, f32[2,16,64,128]{3,2,1,0:T(8,128)} %reshape.73.cos_ref, f32[2,16,64,128]{3,2,1,0:T(8,128)} %reshape.74.sin_ref, ...), custom_call_target="tpu_custom_call" | custom-call | tf_op jit(solution)/shard_map/line/pallas_call | solution.py:247
  112.6 59.9 %all_to_all.10 = f32[256,16,128]{2,1,0:T(8,128)} all-to-all(f32[256,16,128]{2,1,0:T(8,128)} %bitcast.24), channel_id=1, replica_groups=mesh['orient'=2,'slab'=128] {'orient','slab'}, dimensions={0} | all-to-all | bytes 4194304 | tf_op jit(solution)/shard_map/all_to_all | solution.py:261
  172.6 8.1 %close.1 = f32[2,16,128,128]{3,2,1,0:T(8,128)} custom-call(f32[2,2048,128]{2,1,0:T(8,128)} %bitcast.26, f32[128,128]{1,0:T(8,128)} %bitcast.30), custom_call_target="tpu_custom_call" | custom-call | tf_op jit(solution)/shard_map/close/pallas_call | solution.py:262
  (4 shorter events, 0.0 us)
Async XLA Ops:
  21.0 15.7 %copy-start.1 = (f32[3,64]{1,0:T(4,128)S(1)}, f32[3,64]{1,0:T(4,128)}, u32[]{:S(2)}) copy-start(f32[3,64]{1,0:T(4,128)} %param.10) | copy-start | bytes 2308
  21.0 15.9 %copy-start.2 = (f32[64]{0:T(128)S(1)}, f32[64]{0:T(128)}, u32[]{:S(2)}) copy-start(f32[64]{0:T(128)} %param.11) | copy-start | bytes 772
  21.0 68.8 %all-to-all-start = ((f32[256,16,128]{2,1,0:T(8,128)}), f32[256,16,128]{2,1,0:T(8,128)S(1)}, u32[]{:S(2)}, u32[]{:S(2)}) async-start(f32[256,16,128]{2,1,0:T(8,128)} %bitcast.25), calls=%async_computation | async-start | bytes 4194304 | tf_op jit(solution)/shard_map/all_to_all | solution.py:235
  89.9 1.3 copy-start

commit v2 on v1

--- a/solution.py
+++ b/solution.py
@@ -17,7 +17,8 @@
 DECAY_RATE = 0.01
 HIGHEST = lax.Precision.HIGHEST
 AXES = ("orient", "slab")
-INTERPRET = False
+PARAMS = pltpu.CompilerParams(vmem_limit_bytes=24 * 1024 * 1024)
+UNROLL = 4
 
 
 def packed_tables(length):
@@ -36,14 +37,6 @@
     step = HALF_STEP * 2.0 * math.pi / BOX_LENGTH
     angles = components[:, None] * (jnp.arange(length // 2, dtype=jnp.float32) * step)[None, :]
     return jnp.cos(angles), jnp.sin(angles)
-
-
-def shift_kernels(components, length):
-    half = length // 2
-    _, inverse = packed_tables(length)
-    cosines, sines = phase_tables(components, length)
-    sines = jnp.where(jnp.arange(half)[None, :] == 0, 1.0, sines)
-    return jnp.dot(jnp.concatenate([cosines, sines], axis=1), jnp.asarray(inverse.T), precision=HIGHEST)
 
 
 def mixing_matrix(orientations, weights):
@@ -105,27 +98,55 @@
     return pltpu.roll(jnp.broadcast_to(row, (length, length)), 0, 1, stride=1, stride_axis=0)
 
 
-def plane_kernel(propagator_ref, field_ref, kernel_x_ref, kernel_y_ref, out_ref, damping_ref):
-    row = pl.program_id(0)
-    count = pl.num_programs(0)
-
-    @pl.when(row == 0)
+def narrow_product(left, right):
+    left_high, left_low = halves(left)
+    high, low = halves(right)
+    top = jnp.concatenate([high, low], axis=1)
+    bottom = jnp.concatenate([high, jnp.zeros_like(low)], axis=1)
+    both = product(
+        jnp.concatenate([left_high, left_low], axis=1), jnp.concatenate([top, bottom], axis=0)
+    )
+    columns = right.shape[1]
+    return both[:, :columns] + both[:, columns:]
+
+
+def shift_rows(orientations, inverse):
+    length = inverse.shape[0]
+    half = length // 2
+    components = jnp.concatenate([orientations[0:1], -orientations[1:2]], axis=1)
+    orders = lax.broadcasted_iota(jnp.int32, (half, components.shape[1]), 0)
+    angles = components * (orders.astype(jnp.float32) * (HALF_STEP * 2.0 * math.pi / BOX_LENGTH))
+    sines = jnp.where(orders == 0, 1.0, jnp.sin(angles))
+    waves = jnp.concatenate([jnp.cos(angles), sines], axis=0)
+    columns = jnp.dot(inverse, waves, precision=HIGHEST, preferred_element_type=jnp.float32)
+    return columns.T
+
+
+def plane_kernel(count, start, propagator_ref, field_ref, orientations_ref, inverse_ref, out_ref, damping_ref, rows_ref):
+    step = pl.program_id(0)
+    batch = propagator_ref.shape[1]
+    total = rows_ref.shape[0] // 2
+    first_own = start()
+
+    @pl.when(step == 0)
     def _():
         damping_ref[...] = jnp.exp(-0.5 * HALF_STEP * field_ref[...])
-
-    moved = []
-    for part in range(2):
-        own = part * count + row
-        damped = propagator_ref[part, 0] * damping_ref[...]
-        shift_x = circulant(kernel_x_ref[pl.ds(own, 1), :])
-        shift_y = circulant(kernel_y_ref[pl.ds(own, 1), :])
-        along_x = product(wide_left(damped), wide_right(shift_x))
-        moved.append(product(wide_left(shift_y), wide_right(along_x)))
-    first, second = moved
-    low = low_lanes(first.shape)
-    rows = pl.ds(row, first.shape[0], stride=count)
-    out_ref[0, rows, :] = jnp.where(low, first, swap(second))
-    out_ref[1, rows, :] = jnp.where(low, swap(first), second)
+        rows_ref[...] = shift_rows(orientations_ref[...], inverse_ref[...])
+
+    for n in range(batch):
+        row = step * batch + n
+        moved = []
+        for part in range(2):
+            own = first_own + part * count + row
+            damped = propagator_ref[part, n] * damping_ref[...]
+            shift_x = circulant(rows_ref[pl.ds(own, 1), :])
+            shift_y = circulant(rows_ref[pl.ds(total + own, 1), :])
+            moved.append(narrow_product(shift_y, narrow_product(damped, shift_x)))
+        first, second = moved
+        low = low_lanes(first.shape)
+        rows = pl.ds(row, first.shape[0], stride=count)
+        out_ref[0, rows, :] = jnp.where(low, first, swap(second))
+        out_ref[1, rows, :] = jnp.where(low, swap(first), second)
 
 
 def line_kernel(depth, lines_ref, forward_ref, inverse_ref, cos_ref, sin_ref, mixing_ref, out_ref, advected_ref):
@@ -133,6 +154,7 @@
     half = depth // 2
     lanes = lines_ref.shape[2]
     pairs = count // 2
+    pitch = advected_ref.shape[0] // depth
 
     def shift(item, carry):
         group = item // pairs
@@ -147,11 +169,11 @@
         )
         advected = product(inverse_ref[...], wide_right(turned))
         for n in range(2):
-            rows = pl.ds(group * count + row + n, depth, stride=2 * count)
+            rows = pl.ds(group * count + row + n, depth, stride=pitch)
             advected_ref[rows, :] = advected[:, n * lanes : (n + 1) * lanes]
         return carry
 
-    lax.fori_loop(0, 2 * pairs, shift, 0)
+    lax.fori_loop(0, 2 * pairs, shift, 0, unroll=2)
     both = 2 * count
     mixing = wide_left(mixing_ref[...])
     low = low_lanes((both, lanes))
@@ -159,9 +181,9 @@
     def mix(step, carry):
         stacked = []
         for n in range(2):
-            base = (4 * step + 2 * n) * both
+            base = (4 * step + 2 * n) * pitch
             first = advected_ref[pl.ds(base, both), :]
-            second = advected_ref[pl.ds(base + both, both), :]
+            second = advected_ref[pl.ds(base + pitch, both), :]
             stacked.append(
                 jnp.concatenate(
                     [jnp.where(low, first, swap(second)), jnp.where(low, swap(first), second)], axis=0
@@ -179,24 +201,19 @@
                 out_ref[1, target, :] = values[count:]
         return carry
 
-    lax.fori_loop(0, depth // 4, mix, 0)
-
-
-def close_kernel(mixed_ref, field_ref, out_ref, damping_ref):
-    row = pl.program_id(0)
-    count = pl.num_programs(0)
-
-    @pl.when(row == 0)
-    def _():
-        damping_ref[...] = jnp.exp(-0.5 * HALF_STEP * field_ref[...])
-
+    lax.fori_loop(0, depth // 4, mix, 0, unroll=UNROLL)
+
+
+def close_kernel(mixed_ref, field_ref, out_ref):
     depth = field_ref.shape[0]
-    first = mixed_ref[0, pl.ds(row, depth, stride=count), :]
-    second = mixed_ref[1, pl.ds(row, depth, stride=count), :]
-    low = low_lanes(first.shape)
-    damping = damping_ref[...]
-    out_ref[0, 0] = jnp.where(low, first, swap(second)) * damping
-    out_ref[1, 0] = jnp.where(low, swap(first), second) * damping
+    count = out_ref.shape[1]
+    damping = jnp.exp(-0.5 * HALF_STEP * field_ref[...])
+    low = low_lanes(damping.shape)
+    for row in range(count):
+        first = mixed_ref[0, pl.ds(row, depth, stride=count), :]
+        second = mixed_ref[1, pl.ds(row, depth, stride=count), :]
+        out_ref[0, row] = jnp.where(low, first, swap(second)) * damping
+        out_ref[1, row] = jnp.where(low, swap(first), second) * damping
 
 
 def whole(shape):
@@ -210,31 +227,31 @@
     total_z = depth * slabs
     count = own // 2
     half = total_z // 2
-    start = lax.axis_index("orient") * own
-    directions = lax.dynamic_slice_in_dim(orientations, start, own, 1)
-    kernel_x = shift_kernels(directions[0], cols)
-    kernel_y = shift_kernels(-directions[1], rows)
     plane = field[0]
     message = (groups, slabs * count, cols)
+    forward, inverse = packed_tables(total_z)
+    batch = 2
     sent = pl.pallas_call(
-        plane_kernel,
-        grid=(count,),
+        functools.partial(plane_kernel, count, lambda: lax.axis_index("orient") * own),
+        grid=(count // batch,),
         in_specs=[
-            pl.BlockSpec((2, 1, rows, cols), lambda row: (0, row, 0, 0)),
+            pl.BlockSpec((2, batch, rows, cols), lambda row: (0, row, 0, 0)),
             whole((rows, cols)),
-            whole((own, cols)),
-            whole((own, rows)),
+            whole(orientations.shape),
+            whole((cols, cols)),
         ],
         out_specs=whole(message),
         out_shape=jax.ShapeDtypeStruct(message, jnp.float32),
-        scratch_shapes=[pltpu.VMEM((rows, cols), jnp.float32)],
-        interpret=INTERPRET,
+        scratch_shapes=[
+            pltpu.VMEM((rows, cols), jnp.float32),
+            pltpu.VMEM((2 * groups * own, cols), jnp.float32),
+        ],
+        compiler_params=PARAMS,
         name="plane",
-    )(propagator.reshape(2, count, rows, cols), plane, kernel_x, kernel_y)
+    )(propagator.reshape(2, count, rows, cols), plane, orientations, packed_tables(cols)[1])
 
     lines = lax.all_to_all(sent.reshape(groups * slabs, count, cols), AXES, 0, 0, tiled=True)
 
-    forward, inverse = packed_tables(total_z)
     cosines, sines = phase_tables(orientations[2], total_z)
 
     def by_lane(table):
@@ -247,8 +264,8 @@
     back = pl.pallas_call(
         functools.partial(line_kernel, total_z),
         out_shape=jax.ShapeDtypeStruct(message, jnp.float32),
-        scratch_shapes=[pltpu.VMEM((total_z * groups * count, cols), jnp.float32)],
-        interpret=INTERPRET,
+        scratch_shapes=[pltpu.VMEM((total_z * (groups * count + 8), cols), jnp.float32)],
+        compiler_params=PARAMS,
         name="line",
     )(
         lines.reshape(message),
@@ -259,14 +276,17 @@
         matrix,
     )
     mixed = lax.all_to_all(back.reshape(groups * slabs, count, cols), AXES, 0, 0, tiled=True)
+    strip = rows // 4
     result = pl.pallas_call(
         close_kernel,
-        grid=(count,),
-        in_specs=[whole(message), whole((rows, cols))],
-        out_specs=pl.BlockSpec((2, 1, rows, cols), lambda row: (0, row, 0, 0)),
+        grid=(rows // strip,),
+        in_specs=[
+            pl.BlockSpec((groups, strip * count, cols), lambda step: (0, step, 0)),
+            pl.BlockSpec((strip, cols), lambda step: (step, 0)),
+        ],
+        out_specs=pl.BlockSpec((2, count, strip, cols), lambda step: (0, 0, step, 0)),
         out_shape=jax.ShapeDtypeStruct((2, count, rows, cols), jnp.float32),
-        scratch_shapes=[pltpu.VMEM((rows, cols), jnp.float32)],
-        interpret=INTERPRET,
+        compiler_params=PARAMS,
         name="close",
     )(mixed.reshape(message), plane)
     return result.reshape(own, 1, rows, cols)

time: 182 us -> 151 us (0.83)
  Pallas kernels: 44.4 us -> 15.5 us
  local copies, waits for them, and re-layouts: 16.8 us -> 22.7 us
  matrix products: 5.63 us -> 0.3 us
  waiting for transfers between devices: 34.5 us -> 31.9 us
    pallas_call x2, Pallas kernels: 23 us -> 8.29 us  [the longest x1 5.75 us: local(): pl.pallas_call(functools.partial(plane_kernel, count, lambda: lax.axis_in...]
    pallas_call x1, Pallas kernels: 21.4 us -> 7.24 us  [local(): pl.pallas_call(functools.partial(line_kernel, total_z), out_shape=jax.Sha...]
    dot_general x4 -> x0, matrix products: 5.33 us -> none  [shift_kernels(): jnp.dot(jnp.concatenate([cosines, sines], axis=1), jnp.asarray(inverse.T)...]
    unnamed x6 -> x22, local copies, waits for them, and re-layouts: 1.33 us -> 6.51 us
    all_to_all x1, waiting for transfers between devices: 34.5 us -> 31.9 us  [local(): lax.all_to_all(sent.reshape(groups * slabs, count, cols), AXES, 0, 0, til...]
  transfers between devices with their start and end apart: 1 -> 1, of which waited for: 1 -> 1; matrix products, arithmetic and copies ran while one was open for 10% -> 14% of each run, Pallas kernels for 0% -> 0%
where the time goes in v2:
time: 151 us
  blocking collectives  59.6 us (39%)
  waiting for transfers between devices  31.9 us (21%)
  local copies, waits for them, and re-layouts  22.7 us (15%)
  starting transfers between devices  15.6 us (10%)
  Pallas kernels  15.5 us (10%)
  other arithmetic  4.75 us (3%)
    all_to_all x1, blocking collectives, local(): lax.all_to_all(back.reshape(groups * slabs, count, cols), AXES, 0, 0, til...  59.6 us
    all_to_all x1, waiting for transfers between devices, local(): lax.all_to_all(sent.reshape(groups * slabs, count, cols), AXES, 0, 0, til...  31.9 us
    all_to_all x1, starting transfers between devices, local(): lax.all_to_all(sent.reshape(groups * slabs, count, cols), AXES, 0, 0, til...  15.6 us
    broadcast_in_dim x2, local copies, waits for them, and re-layouts, by_lane(): return jnp.repeat(table, cols // 2, axis=3)  8.16 us
    pallas_call x1, Pallas kernels, local(): pl.pallas_call(functools.partial(line_kernel, total_z), out_shape=jax.Sha...  7.24 us
    unnamed x22, local copies, waits for them, and re-layouts  6.51 us
    reshape x2, local copies, waits for them, and re-layouts, by_lane(): return jnp.repeat(table, cols // 2, axis=3)  5.97 us
    pallas_call x1, Pallas kernels, local(): pl.pallas_call(functools.partial(plane_kernel, count, lambda: lax.axis_in...  5.75 us
  transfers between devices with their start and end apart: 1, of which 1 were waited for; matrix products, arithmetic and copies ran while one was open for 14% of the time, Pallas kernels for 0%

profile of v2, /device:TPU:1, one launch (start us, length us, event | category | flops | bytes accessed | tf_op | source)
XLA Modules:
  0.0 150.6 jit_solution(140515299839410490)
XLA Ops:
  0.0 0.0 copy-start.2
  0.0 1.6 %copy-done.2 = f32[32,1,128,128]{3,2,1,0:T(8,128)S(1)} copy-done((f32[32,1,128,128]{3,2,1,0:T(8,128)S(1)}, f32[32,1,128,128]{3,2,1,0:T(8,128)}, u32[]{:S(2)}) %copy-start.2) | copy-done | bytes 2097176
  1.6 0.0 copy-start.3
  1.6 0.8 copy-done.3
  2.4 0.0 copy-start.7
  2.4 0.8 copy-done.7
  3.3 0.0 copy-start.8
  3.3 0.7 copy-done.8
  4.0 5.8 %plane.1 = f32[2,2048,128]{2,1,0:T(8,128)S(1)} custom-call(f32[2,16,128,128]{3,2,1,0:T(8,128)S(1)} %bitcast.19, f32[128,128]{1,0:T(8,128)S(1)} %bitcast.20, f32[3,64]{1,0:T(4,128)S(1)} %copy-done.8, f32[128,128]{1,0:T(8,128)S(1)} %copy-done.7), custom_call_target="tpu_custom_call" | custom-call | tf_op jit(solution)/shard_map/plane/pallas_call | solution.py:234
  9.7 0.0 copy-start
  9.7 1.3 copy-done
  11.0 0.0 copy-start.9
  11.0 15.6 %all-to-all-start = ((f32[256,16,128]{2,1,0:T(8,128)}), f32[256,16,128]{2,1,0:T(8,128)S(1)}, u32[]{:S(2)}, u32[]{:S(2)}) async-start(f32[256,16,128]{2,1,0:T(8,128)} %bitcast.17), calls=%async_computation | async-start | bytes 4194304 | tf_op jit(solution)/shard_map/all_to_all | solution.py:253
  26.7 0.0 copy-done.9
  26.7 0.1 mul.209
  26.8 0.1 copy.8
  26.9 4.7 %multiply_sine_fusion = (f32[2,16,64,2]{3,2,1,0:T(8,128)}, f32[2,16,64,2]{3,2,1,0:T(8,128)S(1)}) fusion(f32[64]{0:T(128)S(1)} %iota_multiply_fusion, f32[2,16,2]{2,1,0:T(8,128)S(1)} %copy.8), kind=kLoop, calls=%fused_computation | loop fusion | flops 4096 | bytes 33280 | tf_op jit(solution)/shard_map/sin | solution.py:39
  31.6 3.4 %broadcast_in_dim.4 = f32[2,16,64,2,64]{4,3,2,1,0:T(2,128)} broadcast(f32[2,16,64,2]{3,2,1,0:T(8,128)S(1)} %get-tuple-element.6), dimensions={0,1,2,3} | broadcast | bytes 1064960 | tf_op jit(solution)/shard_map/broadcast_in_dim | solution.py:259
  35.1 2.6 %reshape.61.cos_ref = f32[2,16,64,128]{3,2,1,0:T(8,128)S(1)} reshape(f32[2,16,64,2,64]{4,3,2,1,0:T(2,128)} %broadcast_in_dim.4) | data formatting | bytes 2097152 | tf_op jit(solution)/shard_map/reshape | solution.py:259
  37.6 4.8 %broadcast_in_dim.10 = f32[2,16,64,2,64]{4,3,2,1,0:T(2,128)} broadcast(f32[2,16,64,2]{3,2,1,0:T(8,128)} %get-tuple-element.5), dimensions={0,1,2,3} | broadcast | bytes 1064960 | tf_op jit(solution)/shard_map/broadcast_in_dim | solution.py:259
  42.4 0.0 copy-start.10
  42.4 0.0 copy-start.5
  42.4 0.0 copy-start.6
  42.4 3.4 %reshape.62.sin_ref = f32[2,16,64,128]{3,2,1,0:T(8,128)} reshape(f32[2,16,64,2,64]{4,3,2,1,0:T(2,128)} %broadcast_in_dim.10) | data formatting | bytes 2097152 | tf_op jit(solution)/shard_map/reshape | solution.py:259
  45.8 0.0 copy-done.10
  45.8 0.3 add_multiply_fusion
  46.1 0.2 reshape.63
  46.3 0.7 copy.12
  47.0 1.1 reshape.64.mixing_ref
  48.0 31.9 %all-to-all-done = f32[256,16,128]{2,1,0:T(8,128)S(1)} async-done(((f32[256,16,128]{2,1,0:T(8,128)}), f32[256,16,128]{2,1,0:T(8,128)S(1)}, u32[]{:S(2)}, u32[]{:S(2)}) %all-to-all-start) | async-done | bytes 2097184 | tf_op jit(solution)/shard_map/all_to_all | solution.py:253
  79.9 0.0 copy-done.5
  79.9 0.0 copy-done.6
  79.9 0.0 copy-start.1
  79.9 1.2 copy-done.1
  81.1 7.2 %line.1 = f32[2,2048,128]{2,1,0:T(8,128)S(1)} custom-call(f32[2,2048,128]{2,1,0:T(8,128)S(1)} %bitcast.15, bf16[128,384]{1,0:T(8,128)(2,1)S(1)} %copy-done.5, bf16[128,384]{1,0:T(8,128)(2,1)S(1)} %copy-done.6, f32[2,16,64,128]{3,2,1,0:T(8,128)S(1)} %reshape.61.cos_ref, f32[2,16,64,128]{3,2,1,0:T(8,128)S(1)} %copy-done.1, f32[64,64]{1,0:T(8,128)S(1)} %reshape.64.mixing_ref), custom_call_target="tpu_custom_call" | custom-call | tf_op jit(solution)/shard_map/line/pallas_call | solution.py:264
  88.4 0.0 copy-start.4
  88.4 59.6 %all_to_all.10 = f32[256,16,128]{2,1,0:T(8,128)S(1)} all-to-all(f32[256,16,128]{2,1,0:T(8,128)S(1)} %bitcast.16), channel_id=1, replica_groups=mesh['orient'=2,'slab'=128] {'orient','slab'}, dimensions={0} | all-to-all | bytes 4194304 | tf_op jit(solution)/shard_map/all_to_all | solution.py:278
  148.0 0.0 copy-done.4
  148.0 2.5 %close.1 = f32[2,16,128,128]{3,2,1,0:T(8,128)} custom-call(f32[2,2048,128]{2,1,0:T(8,128)S(1)} %bitcast.18, f32[128,128]{1,0:T(8,128)S(1)} %bitcast.21), custom_call_target="tpu_custom_call" | custom-call | tf_op jit(solution)/shard_map/close/pallas_call | solution.py:280
  (2 shorter events, 0.0 us)
Async XLA Ops:
  0.0 1.6 %copy-start.2 = (f32[32,1,128,128]{3,2,1,0:T(8,128)S(1)}, f32[32,1,128,128]{3,2,1,0:T(8,128)}, u32[]{:S(2)}) copy-start(f32[32,1,128,128]{3,2,1,0:T(8,128)} %param.7) | copy-start | bytes 6291460
  1.6 0.8 copy-start.3
  2.4 0.8 copy-start.7
  3.3 0.7 copy-start.8
  9.7 1.3 copy-start
  11.0 15.7 %copy-start.9 = (f32[3,64]{1,0:T(4,128)S(1)}, f32[3,64]{1,0:T(4,128)}, u32[]{:S(2)}) copy-start(f32[3,64]{1,0:T(4,128)} %orientations_ref.1) | copy-start | bytes 2308
  11.0 68.8 %all-to-all-start = ((f32[256,16,128]{2,1,0:T(8,128)}), f32[256,16,128]{2,1,0:T(8,128)S(1)}, u32[]{:S(2)}, u32[]{:S(2)}) async-start(f32[256,16,128]{2,1,0:T(8,128)} %bitcast.17), calls=%async_computation | async-start | bytes 4194304 | tf_op jit(solution)/shard_map/all_to_all | solution.py:253
  42.4 3.4 %copy-start.10 = (f32[64]{0:T(128)S(1)}, f32[64]{0:T(128)}, u32[]{:S(2)}) copy-start(f32[64]{0:T(128)} %param.10) | copy-start | bytes 772
  42.4 37.5 %copy-start.5 = (bf16[128,384]{1,0:T(8,128)(2,1)S(1)}, bf16[128,384]{1,0:T(8,128)(2,1)}, u32[]{:S(2)}) copy-start(bf16[128,384]{1,0:T(8,128)(2,1)} %constant.98.clone.forward_ref) | copy-start | bytes 294916
  42.4 37.5 %copy-start.6 = (bf16[128,384]{1,0:T(8,128)(2,1)S(1)}, bf16[128,384]{1,0:T(8,128)(2,1)}, u32[]{:S(2)}) copy-start(bf16[128,384]{1,0:T(8,128)(2,1)} %constant.99.clone.inverse_ref) | copy-start | bytes 294916
  79.9 1.2 copy-start.1
  88.4 59.6 %copy-start.4 = (f32[1,128,128]{2,1,0:T(8,128)S(1)}, f32[1,128,128]{2,1,0:T(8,128)}, u32[]{:S(2)}) copy-start(f32[1,128,128]{2,1,0:T(8,128)} %param.8) | copy-start | bytes 196612

commit v3 on v2

--- a/solution.py
+++ b/solution.py
@@ -17,8 +17,11 @@
 DECAY_RATE = 0.01
 HIGHEST = lax.Precision.HIGHEST
 AXES = ("orient", "slab")
-PARAMS = pltpu.CompilerParams(vmem_limit_bytes=24 * 1024 * 1024)
-UNROLL = 4
+SMALL = pltpu.CompilerParams(vmem_limit_bytes=16 * 1024 * 1024)
+LARGE = pltpu.CompilerParams()
+BATCH = 8
+SHIFT_UNROLL = 8
+MIX_UNROLL = 16
 
 
 def packed_tables(length):
@@ -31,12 +34,6 @@
     forward = np.concatenate([np.cos(angles), sines], axis=1)
     scale = np.where(np.arange(length) % half == 0, 1.0, 2.0) / length
     return forward.astype(np.float32), (forward * scale[None, :]).astype(np.float32)
-
-
-def phase_tables(components, length):
-    step = HALF_STEP * 2.0 * math.pi / BOX_LENGTH
-    angles = components[:, None] * (jnp.arange(length // 2, dtype=jnp.float32) * step)[None, :]
-    return jnp.cos(angles), jnp.sin(angles)
 
 
 def mixing_matrix(orientations, weights):
@@ -173,7 +170,7 @@
             advected_ref[rows, :] = advected[:, n * lanes : (n + 1) * lanes]
         return carry
 
-    lax.fori_loop(0, 2 * pairs, shift, 0, unroll=2)
+    lax.fori_loop(0, 2 * pairs, shift, 0, unroll=SHIFT_UNROLL)
     both = 2 * count
     mixing = wide_left(mixing_ref[...])
     low = low_lanes((both, lanes))
@@ -201,7 +198,25 @@
                 out_ref[1, target, :] = values[count:]
         return carry
 
-    lax.fori_loop(0, depth // 4, mix, 0, unroll=UNROLL)
+    lax.fori_loop(0, depth // 4, mix, 0, unroll=MIX_UNROLL)
+
+
+def phase_kernel(orientations_ref, cos_ref, sin_ref):
+    groups, count, half, lanes = cos_ref.shape
+    component = orientations_ref[2:3, :]
+    orders = lax.broadcasted_iota(jnp.int32, (half, component.shape[1]), 0)
+    angles = component * (orders.astype(jnp.float32) * (HALF_STEP * 2.0 * math.pi / BOX_LENGTH))
+    low = low_lanes((half, lanes))
+    for table, out_ref in ((jnp.cos(angles), cos_ref), (jnp.sin(angles), sin_ref)):
+        for group in range(groups):
+            for row in range(count):
+                first = 2 * count * group + row
+                second = first + count
+                out_ref[group, row] = jnp.where(
+                    low,
+                    jnp.broadcast_to(table[:, first : first + 1], (half, lanes)),
+                    jnp.broadcast_to(table[:, second : second + 1], (half, lanes)),
+                )
 
 
 def close_kernel(mixed_ref, field_ref, out_ref):
@@ -220,22 +235,14 @@
     return pl.BlockSpec(shape, lambda row: (0,) * len(shape))
 
 
-def local(propagator, field, orientations, weights):
-    own, depth, rows, cols = propagator.shape
-    groups = lax.axis_size("orient")
-    slabs = lax.axis_size("slab")
-    total_z = depth * slabs
-    count = own // 2
-    half = total_z // 2
-    plane = field[0]
-    message = (groups, slabs * count, cols)
-    forward, inverse = packed_tables(total_z)
-    batch = 2
-    sent = pl.pallas_call(
-        functools.partial(plane_kernel, count, lambda: lax.axis_index("orient") * own),
-        grid=(count // batch,),
+def run_plane(propagator, plane, orientations, start):
+    _, count, rows, cols = propagator.shape
+    message = (2, rows * count, cols)
+    return pl.pallas_call(
+        functools.partial(plane_kernel, count, start),
+        grid=(count // BATCH,),
         in_specs=[
-            pl.BlockSpec((2, batch, rows, cols), lambda row: (0, row, 0, 0)),
+            pl.BlockSpec((2, BATCH, rows, cols), lambda row: (0, row, 0, 0)),
             whole((rows, cols)),
             whole(orientations.shape),
             whole((cols, cols)),
@@ -244,40 +251,38 @@
         out_shape=jax.ShapeDtypeStruct(message, jnp.float32),
         scratch_shapes=[
             pltpu.VMEM((rows, cols), jnp.float32),
-            pltpu.VMEM((2 * groups * own, cols), jnp.float32),
+            pltpu.VMEM((2 * orientations.shape[1], cols), jnp.float32),
         ],
-        compiler_params=PARAMS,
+        compiler_params=LARGE,
         name="plane",
-    )(propagator.reshape(2, count, rows, cols), plane, orientations, packed_tables(cols)[1])
-
-    lines = lax.all_to_all(sent.reshape(groups * slabs, count, cols), AXES, 0, 0, tiled=True)
-
-    cosines, sines = phase_tables(orientations[2], total_z)
-
-    def by_lane(table):
-        table = table.reshape(groups, 2, count, half).transpose(0, 2, 3, 1)
-        return jnp.repeat(table, cols // 2, axis=3)
-
-    matrix = mixing_matrix(orientations, weights)
-    matrix = matrix.reshape(groups, 2, count, groups, 2, count).transpose(1, 0, 2, 4, 3, 5)
-    matrix = matrix.reshape(2 * own, 2 * own)
-    back = pl.pallas_call(
+    )(propagator, plane, orientations, packed_tables(cols)[1])
+
+
+def run_phase(orientations, groups, count, half, lanes):
+    shape = jax.ShapeDtypeStruct((groups, count, half, lanes), jnp.float32)
+    return pl.pallas_call(
+        phase_kernel, out_shape=(shape, shape), compiler_params=SMALL, name="phase"
+    )(orientations)
+
+
+def run_line(lines, cosines, sines, matrix, total_z):
+    groups, height, cols = lines.shape
+    forward, inverse = packed_tables(total_z)
+    pitch = groups * (height // total_z) + 8
+    return pl.pallas_call(
         functools.partial(line_kernel, total_z),
-        out_shape=jax.ShapeDtypeStruct(message, jnp.float32),
-        scratch_shapes=[pltpu.VMEM((total_z * (groups * count + 8), cols), jnp.float32)],
-        compiler_params=PARAMS,
+        out_shape=jax.ShapeDtypeStruct(lines.shape, jnp.float32),
+        scratch_shapes=[pltpu.VMEM((total_z * pitch, cols), jnp.float32)],
+        compiler_params=SMALL,
         name="line",
-    )(
-        lines.reshape(message),
-        wide_table(forward.T),
-        wide_table(inverse),
-        by_lane(cosines),
-        by_lane(sines),
-        matrix,
-    )
-    mixed = lax.all_to_all(back.reshape(groups * slabs, count, cols), AXES, 0, 0, tiled=True)
+    )(lines, wide_table(forward.T), wide_table(inverse), cosines, sines, matrix)
+
+
+def run_close(mixed, plane, count):
+    groups = mixed.shape[0]
+    rows, cols = plane.shape
     strip = rows // 4
-    result = pl.pallas_call(
+    return pl.pallas_call(
         close_kernel,
         grid=(rows // strip,),
         in_specs=[
@@ -286,9 +291,29 @@
         ],
         out_specs=pl.BlockSpec((2, count, strip, cols), lambda step: (0, 0, step, 0)),
         out_shape=jax.ShapeDtypeStruct((2, count, rows, cols), jnp.float32),
-        compiler_params=PARAMS,
+        compiler_params=SMALL,
         name="close",
-    )(mixed.reshape(message), plane)
+    )(mixed, plane)
+
+
+def local(propagator, field, orientations, weights):
+    own, depth, rows, cols = propagator.shape
+    groups = lax.axis_size("orient")
+    slabs = lax.axis_size("slab")
+    total_z = depth * slabs
+    count = own // 2
+    plane = field[0]
+    sent = run_plane(
+        propagator.reshape(2, count, rows, cols), plane, orientations, lambda: lax.axis_index("orient") * own
+    )
+    lines = lax.all_to_all(sent.reshape(groups * slabs, count, cols), AXES, 0, 0, tiled=True)
+    cosines, sines = run_phase(orientations, groups, count, total_z // 2, cols)
+    matrix = mixing_matrix(orientations, weights)
+    matrix = matrix.reshape(groups, 2, count, groups, 2, count).transpose(1, 0, 2, 4, 3, 5)
+    matrix = matrix.reshape(2 * own, 2 * own)
+    back = run_line(lines.reshape(sent.shape), cosines, sines, matrix, total_z)
+    mixed = lax.all_to_all(back.reshape(groups * slabs, count, cols), AXES, 0, 0, tiled=True)
+    result = run_close(mixed.reshape(sent.shape), plane, count)
     return result.reshape(own, 1, rows, cols)
 
 

time: 151 us -> 142 us (0.940)
  local copies, waits for them, and re-layouts: 22.7 us -> 4.14 us
  waiting for transfers between devices: 31.9 us -> 48.5 us
  other arithmetic: 4.75 us -> 0 us
  Pallas kernels: 15.5 us -> 13.4 us
    all_to_all x1, waiting for transfers between devices: 31.9 us -> 48.5 us  [local(): lax.all_to_all(sent.reshape(groups * slabs, count, cols), AXES, 0, 0, til...]
    broadcast_in_dim x2 -> x0, local copies, waits for them, and re-layouts: 8.16 us -> none  [by_lane(): return jnp.repeat(table, cols // 2, axis=3)]
    reshape x2 -> x0, local copies, waits for them, and re-layouts: 5.97 us -> none  [by_lane(): return jnp.repeat(table, cols // 2, axis=3)]
    sin x1 -> x0, other arithmetic: 4.74 us -> none  [phase_tables(): return (jnp.cos(angles), jnp.sin(angles))]
    unnamed x22 -> x14, local copies, waits for them, and re-layouts: 6.51 us -> 2.21 us
    pallas_call x3 -> x4, Pallas kernels: 15.5 us -> 13.4 us  [the longest x1 5.56 us: run_plane(): pl.pallas_call(functools.partial(plane_kernel, count, start), grid=(count...]
  transfers between devices with their start and end apart: 1 -> 1, of which waited for: 1 -> 1; matrix products, arithmetic and copies ran while one was open for 14% -> 2% of each run, Pallas kernels for 0% -> 1%
where the time goes in v3:
time: 142 us
  blocking collectives  59.6 us (42%)
  waiting for transfers between devices  48.5 us (34%)
  starting transfers between devices  15.7 us (11%)
  Pallas kernels  13.4 us (9%)
  local copies, waits for them, and re-layouts  4.14 us (3%)
    all_to_all x1, blocking collectives, local(): lax.all_to_all(back.reshape(groups * slabs, count, cols), AXES, 0, 0, til...  59.6 us
    all_to_all x1, waiting for transfers between devices, local(): lax.all_to_all(sent.reshape(groups * slabs, count, cols), AXES, 0, 0, til...  48.5 us
    all_to_all x1, starting transfers between devices, local(): lax.all_to_all(sent.reshape(groups * slabs, count, cols), AXES, 0, 0, til...  15.7 us
    pallas_call x1, Pallas kernels, run_plane(): pl.pallas_call(functools.partial(plane_kernel, count, start), grid=(count...  5.56 us
    pallas_call x1, Pallas kernels, run_line(): pl.pallas_call(functools.partial(line_kernel, total_z), out_shape=jax.Sha...  3.84 us
  transfers between devices with their start and end apart: 1, of which 1 were waited for; matrix products, arithmetic and copies ran while one was open for 2% of the time, Pallas kernels for 1%

profile of v3, /device:TPU:1, one launch (start us, length us, event | category | flops | bytes accessed | tf_op | source)
XLA Modules:
  0.0 141.7 jit_solution(6857591793143633861)
XLA Ops:
  0.0 5.6 %plane.1 = f32[2,2048,128]{2,1,0:T(8,128)} custom-call(f32[2,16,128,128]{3,2,1,0:T(8,128)} %bitcast.20, f32[128,128]{1,0:T(8,128)} %bitcast.17, f32[3,64]{1,0:T(4,128)} %orientations_ref.3, f32[128,128]{1,0:T(8,128)} %constant.95.clone.inverse_ref), custom_call_target="tpu_custom_call" | custom-call | tf_op jit(solution)/shard_map/plane/pallas_call | solution.py:241
  5.6 0.0 copy-start.5
  5.6 0.0 copy-start.6
  5.6 0.0 copy-start.3
  5.6 0.0 copy-start.4
  5.6 15.7 %all-to-all-start = ((f32[256,16,128]{2,1,0:T(8,128)}), f32[256,16,128]{2,1,0:T(8,128)S(1)}, u32[]{:S(2)}, u32[]{:S(2)}) async-start(f32[256,16,128]{2,1,0:T(8,128)} %bitcast.19), calls=%async_computation | async-start | bytes 4194304 | tf_op jit(solution)/shard_map/all_to_all | solution.py:309
  21.2 0.0 copy-done.5
  21.3 1.5 %phase.1 = (f32[2,16,64,128]{3,2,1,0:T(8,128)S(1)}, f32[2,16,64,128]{3,2,1,0:T(8,128)S(1)}) custom-call(f32[3,64]{1,0:T(4,128)S(1)} %copy-done.5), custom_call_target="tpu_custom_call" | custom-call | tf_op jit(solution)/shard_map/phase/pallas_call | solution.py:263
  22.7 0.0 copy-start
  22.7 1.0 copy-done
  23.7 0.0 copy-done.6
  23.7 0.3 add_multiply_fusion
  24.0 0.2 reshape.28
  24.2 0.7 copy.11
  24.9 1.1 reshape.29.mixing_ref
  25.9 48.5 %all-to-all-done = f32[256,16,128]{2,1,0:T(8,128)S(1)} async-done(((f32[256,16,128]{2,1,0:T(8,128)}), f32[256,16,128]{2,1,0:T(8,128)S(1)}, u32[]{:S(2)}, u32[]{:S(2)}) %all-to-all-start) | async-done | bytes 2097184 | tf_op jit(solution)/shard_map/all_to_all | solution.py:309
  74.4 0.0 copy-done.3
  74.4 0.0 copy-done.4
  74.4 0.0 copy-start.1
  74.4 1.2 copy-done.1
  75.7 3.8 %line.1 = f32[2,2048,128]{2,1,0:T(8,128)S(1)} custom-call(f32[2,2048,128]{2,1,0:T(8,128)S(1)} %bitcast.14, bf16[128,384]{1,0:T(8,128)(2,1)S(1)} %copy-done.4, bf16[128,384]{1,0:T(8,128)(2,1)S(1)} %copy-done.3, f32[2,16,64,128]{3,2,1,0:T(8,128)S(1)} %get-tuple-element.7.cos_ref, f32[2,16,64,128]{3,2,1,0:T(8,128)S(1)} %copy-done.1, ...), custom_call_target="tpu_custom_call" | custom-call | tf_op jit(solution)/shard_map/line/pallas_call | solution.py:272
  79.5 0.0 copy-start.2
  79.5 59.6 %all_to_all.10 = f32[256,16,128]{2,1,0:T(8,128)S(1)} all-to-all(f32[256,16,128]{2,1,0:T(8,128)S(1)} %bitcast.15), channel_id=1, replica_groups=mesh['orient'=2,'slab'=128] {'orient','slab'}, dimensions={0} | all-to-all | bytes 4194304 | tf_op jit(solution)/shard_map/all_to_all | solution.py:315
  139.2 0.0 copy-done.2
  139.2 2.5 %close.1 = f32[2,16,128,128]{3,2,1,0:T(8,128)} custom-call(f32[2,2048,128]{2,1,0:T(8,128)S(1)} %bitcast.16, f32[128,128]{1,0:T(8,128)S(1)} %bitcast.18), custom_call_target="tpu_custom_call" | custom-call | tf_op jit(solution)/shard_map/close/pallas_call | solution.py:285
Async XLA Ops:
  5.6 15.7 %copy-start.5 = (f32[3,64]{1,0:T(4,128)S(1)}, f32[3,64]{1,0:T(4,128)}, u32[]{:S(2)}) copy-start(f32[3,64]{1,0:T(4,128)} %orientations_ref.3) | copy-start | bytes 2308
  5.6 18.1 %copy-start.6 = (f32[64]{0:T(128)S(1)}, f32[64]{0:T(128)}, u32[]{:S(2)}) copy-start(f32[64]{0:T(128)} %param.10) | copy-start | bytes 772
  5.6 68.9 %copy-start.3 = (bf16[128,384]{1,0:T(8,128)(2,1)S(1)}, bf16[128,384]{1,0:T(8,128)(2,1)}, u32[]{:S(2)}) copy-start(bf16[128,384]{1,0:T(8,128)(2,1)} %constant.97.clone.inverse_ref) | copy-start | bytes 294916
  5.6 68.9 %copy-start.4 = (bf16[128,384]{1,0:T(8,128)(2,1)S(1)}, bf16[128,384]{1,0:T(8,128)(2,1)}, u32[]{:S(2)}) copy-start(bf16[128,384]{1,0:T(8,128)(2,1)} %constant.96.clone.forward_ref) | copy-start | bytes 294916
  5.6 68.9 %all-to-all-start = ((f32[256,16,128]{2,1,0:T(8,128)}), f32[256,16,128]{2,1,0:T(8,128)S(1)}, u32[]{:S(2)}, u32[]{:S(2)}) async-start(f32[256,16,128]{2,1,0:T(8,128)} %bitcast.19), calls=%async_computation | async-start | bytes 4194304 | tf_op jit(solution)/shard_map/all_to_all | solution.py:309
  22.7 1.0 copy-start
  74.4 1.2 copy-start.1
  79.5 59.6 %copy-start.2 = (f32[1,128,128]{2,1,0:T(8,128)S(1)}, f32[1,128,128]{2,1,0:T(8,128)}, u32[]{:S(2)}) copy-start(f32[1,128,128]{2,1,0:T(8,128)} %param.8) | copy-start | bytes 196612

commit v4 on v3

--- a/solution.py
+++ b/solution.py
@@ -20,8 +20,8 @@
 SMALL = pltpu.CompilerParams(vmem_limit_bytes=16 * 1024 * 1024)
 LARGE = pltpu.CompilerParams()
 BATCH = 8
-SHIFT_UNROLL = 8
-MIX_UNROLL = 16
+STRIPS = 2
+MIX_UNROLL = 32
 
 
 def packed_tables(length):
@@ -146,31 +146,38 @@
         out_ref[1, rows, :] = jnp.where(low, swap(first), second)
 
 
-def line_kernel(depth, lines_ref, forward_ref, inverse_ref, cos_ref, sin_ref, mixing_ref, out_ref, advected_ref):
+def line_kernel(depth, lines_ref, forward_ref, inverse_ref, phases_ref, mixing_ref, out_ref, advected_ref):
+    groups = lines_ref.shape[0]
     count = lines_ref.shape[1] // depth
     half = depth // 2
     lanes = lines_ref.shape[2]
-    pairs = count // 2
     pitch = advected_ref.shape[0] // depth
-
-    def shift(item, carry):
-        group = item // pairs
-        row = 2 * (item % pairs)
-        taken = [lines_ref[group, pl.ds(row + n, depth, stride=count), :] for n in range(2)]
-        spectrum = product(forward_ref[...], wide_right(jnp.concatenate(taken, axis=1)))
-        cosines = jnp.concatenate([cos_ref[group, row + n] for n in range(2)], axis=1)
-        sines = jnp.concatenate([sin_ref[group, row + n] for n in range(2)], axis=1)
-        real, imaginary = spectrum[:half], spectrum[half:]
-        turned = jnp.concatenate(
-            [real * cosines - imaginary * sines, real * sines + imaginary * cosines], axis=0
+    quarter = lanes // 4
+    even = (lax.broadcasted_iota(jnp.int32, (half, lanes), 1) // quarter) % 2 == 0
+
+    def spread(group, row):
+        packed = phases_ref[group, row]
+        return (
+            jnp.where(even, packed, pltpu.roll(packed, quarter, 1)),
+            jnp.where(even, pltpu.roll(packed, lanes - quarter, 1), packed),
         )
-        advected = product(inverse_ref[...], wide_right(turned))
-        for n in range(2):
-            rows = pl.ds(group * count + row + n, depth, stride=pitch)
-            advected_ref[rows, :] = advected[:, n * lanes : (n + 1) * lanes]
-        return carry
-
-    lax.fori_loop(0, 2 * pairs, shift, 0, unroll=SHIFT_UNROLL)
+
+    for group in range(groups):
+        for row in range(0, count, 2):
+            taken = [lines_ref[group, pl.ds(row + n, depth, stride=count), :] for n in range(2)]
+            spectrum = product(forward_ref[...], wide_right(jnp.concatenate(taken, axis=1)))
+            cosines, sines = (
+                jnp.concatenate(tables, axis=1) for tables in zip(*(spread(group, row + n) for n in range(2)))
+            )
+            real, imaginary = spectrum[:half], spectrum[half:]
+            turned = jnp.concatenate(
+                [real * cosines - imaginary * sines, real * sines + imaginary * cosines], axis=0
+            )
+            advected = product(inverse_ref[...], wide_right(turned))
+            for n in range(2):
+                rows = pl.ds(group * count + row + n, depth, stride=pitch)
+                advected_ref[rows, :] = advected[:, n * lanes : (n + 1) * lanes]
+
     both = 2 * count
     mixing = wide_left(mixing_ref[...])
     low = low_lanes((both, lanes))
@@ -201,32 +208,36 @@
     lax.fori_loop(0, depth // 4, mix, 0, unroll=MIX_UNROLL)
 
 
-def phase_kernel(orientations_ref, cos_ref, sin_ref):
-    groups, count, half, lanes = cos_ref.shape
+def phase_kernel(orientations_ref, out_ref):
+    groups, count, half, lanes = out_ref.shape
     component = orientations_ref[2:3, :]
     orders = lax.broadcasted_iota(jnp.int32, (half, component.shape[1]), 0)
     angles = component * (orders.astype(jnp.float32) * (HALF_STEP * 2.0 * math.pi / BOX_LENGTH))
-    low = low_lanes((half, lanes))
-    for table, out_ref in ((jnp.cos(angles), cos_ref), (jnp.sin(angles), sin_ref)):
-        for group in range(groups):
-            for row in range(count):
-                first = 2 * count * group + row
-                second = first + count
-                out_ref[group, row] = jnp.where(
-                    low,
-                    jnp.broadcast_to(table[:, first : first + 1], (half, lanes)),
-                    jnp.broadcast_to(table[:, second : second + 1], (half, lanes)),
-                )
+    cosines, sines = jnp.cos(angles), jnp.sin(angles)
+    quarters = lax.broadcasted_iota(jnp.int32, (half, lanes), 1) // (lanes // 4)
+    for group in range(groups):
+        for row in range(count):
+            first = 2 * count * group + row
+            values = [
+                jnp.broadcast_to(table[:, n : n + 1], (half, lanes))
+                for n in (first, first + count)
+                for table in (cosines, sines)
+            ]
+            low = jnp.where(quarters == 0, values[0], values[1])
+            high = jnp.where(quarters == 2, values[2], values[3])
+            out_ref[group, row] = jnp.where(quarters < 2, low, high)
 
 
 def close_kernel(mixed_ref, field_ref, out_ref):
-    depth = field_ref.shape[0]
+    depth = out_ref.shape[2]
     count = out_ref.shape[1]
-    damping = jnp.exp(-0.5 * HALF_STEP * field_ref[...])
+    base = pl.program_id(0) * depth
+    damping = jnp.exp(-0.5 * HALF_STEP * field_ref[pl.ds(base, depth), :])
     low = low_lanes(damping.shape)
     for row in range(count):
-        first = mixed_ref[0, pl.ds(row, depth, stride=count), :]
-        second = mixed_ref[1, pl.ds(row, depth, stride=count), :]
+        rows = pl.ds(base * count + row, depth, stride=count)
+        first = mixed_ref[0, rows, :]
+        second = mixed_ref[1, rows, :]
         out_ref[0, row] = jnp.where(low, first, swap(second)) * damping
         out_ref[1, row] = jnp.where(low, swap(first), second) * damping
 
@@ -261,11 +272,11 @@
 def run_phase(orientations, groups, count, half, lanes):
     shape = jax.ShapeDtypeStruct((groups, count, half, lanes), jnp.float32)
     return pl.pallas_call(
-        phase_kernel, out_shape=(shape, shape), compiler_params=SMALL, name="phase"
+        phase_kernel, out_shape=shape, compiler_params=SMALL, name="phase"
     )(orientations)
 
 
-def run_line(lines, cosines, sines, matrix, total_z):
+def run_line(lines, phases, matrix, total_z):
     groups, height, cols = lines.shape
     forward, inverse = packed_tables(total_z)
     pitch = groups * (height // total_z) + 8
@@ -275,20 +286,16 @@
         scratch_shapes=[pltpu.VMEM((total_z * pitch, cols), jnp.float32)],
         compiler_params=SMALL,
         name="line",
-    )(lines, wide_table(forward.T), wide_table(inverse), cosines, sines, matrix)
+    )(lines, wide_table(forward.T), wide_table(inverse), phases, matrix)
 
 
 def run_close(mixed, plane, count):
-    groups = mixed.shape[0]
     rows, cols = plane.shape
-    strip = rows // 4
+    strip = rows // STRIPS
     return pl.pallas_call(
         close_kernel,
         grid=(rows // strip,),
-        in_specs=[
-            pl.BlockSpec((groups, strip * count, cols), lambda step: (0, step, 0)),
-            pl.BlockSpec((strip, cols), lambda step: (step, 0)),
-        ],
+        in_specs=[pl.BlockSpec(memory_space=pltpu.VMEM)] * 2,
         out_specs=pl.BlockSpec((2, count, strip, cols), lambda step: (0, 0, step, 0)),
         out_shape=jax.ShapeDtypeStruct((2, count, rows, cols), jnp.float32),
         compiler_params=SMALL,
@@ -307,11 +314,11 @@
         propagator.reshape(2, count, rows, cols), plane, orientations, lambda: lax.axis_index("orient") * own
     )
     lines = lax.all_to_all(sent.reshape(groups * slabs, count, cols), AXES, 0, 0, tiled=True)
-    cosines, sines = run_phase(orientations, groups, count, total_z // 2, cols)
+    phases = run_phase(orientations, groups, count, total_z // 2, cols)
     matrix = mixing_matrix(orientations, weights)
     matrix = matrix.reshape(groups, 2, count, groups, 2, count).transpose(1, 0, 2, 4, 3, 5)
     matrix = matrix.reshape(2 * own, 2 * own)
-    back = run_line(lines.reshape(sent.shape), cosines, sines, matrix, total_z)
+    back = run_line(lines.reshape(sent.shape), phases, matrix, total_z)
     mixed = lax.all_to_all(back.reshape(groups * slabs, count, cols), AXES, 0, 0, tiled=True)
     result = run_close(mixed.reshape(sent.shape), plane, count)
     return result.reshape(own, 1, rows, cols)

time: 142 us -> 139 us (0.979)
  local copies, waits for them, and re-layouts: 4.14 us -> 1.95 us
    unnamed x14 -> x10, local copies, waits for them, and re-layouts: 2.21 us -> 0.03 us
where the time goes in v4:
time: 139 us
  blocking collectives  59.6 us (43%)
  waiting for transfers between devices  49.6 us (36%)
  starting transfers between devices  15.6 us (11%)
  Pallas kernels  12 us (9%)
  local copies, waits for them, and re-layouts  1.95 us (1%)
    all_to_all x1, blocking collectives, local(): lax.all_to_all(back.reshape(groups * slabs, count, cols), AXES, 0, 0, til...  59.6 us
    all_to_all x1, waiting for transfers between devices, local(): lax.all_to_all(sent.reshape(groups * slabs, count, cols), AXES, 0, 0, til...  49.6 us
    all_to_all x1, starting transfers between devices, local(): lax.all_to_all(sent.reshape(groups * slabs, count, cols), AXES, 0, 0, til...  15.6 us
    pallas_call x1, Pallas kernels, run_plane(): pl.pallas_call(functools.partial(plane_kernel, count, start), grid=(count...  5.56 us
    pallas_call x1, Pallas kernels, run_line(): pl.pallas_call(functools.partial(line_kernel, total_z), out_shape=jax.Sha...  2.99 us
  transfers between devices with their start and end apart: 1, of which 1 were waited for; matrix products, arithmetic and copies ran while one was open for 2% of the time, Pallas kernels for 1%

profile of v4, /device:TPU:1, one launch (start us, length us, event | category | flops | bytes accessed | tf_op | source)
XLA Modules:
  0.0 139.1 jit_solution(7862098195381106306)
XLA Ops:
  0.0 5.6 %plane.1 = f32[2,2048,128]{2,1,0:T(8,128)} custom-call(f32[2,16,128,128]{3,2,1,0:T(8,128)} %bitcast.20, f32[128,128]{1,0:T(8,128)} %bitcast.17, f32[3,64]{1,0:T(4,128)} %orientations_ref.3, f32[128,128]{1,0:T(8,128)} %constant.95.clone.inverse_ref), custom_call_target="tpu_custom_call" | custom-call | tf_op jit(solution)/shard_map/plane/pallas_call | solution.py:252
  5.6 0.0 copy-start.3
  5.6 0.0 copy-start.4
  5.6 15.6 %all-to-all-start = ((f32[256,16,128]{2,1,0:T(8,128)}), f32[256,16,128]{2,1,0:T(8,128)S(1)}, u32[]{:S(2)}, u32[]{:S(2)}) async-start(f32[256,16,128]{2,1,0:T(8,128)} %bitcast.19), calls=%async_computation | async-start | bytes 4194304 | tf_op jit(solution)/shard_map/all_to_all | solution.py:316
  21.2 0.0 copy-done.3
  21.2 0.0 copy-start.1
  21.2 0.0 copy-start.2
  21.3 1.3 phase.1.phases_ref
  22.6 0.0 copy-done.4
  22.6 0.3 add_multiply_fusion
  22.9 0.2 reshape.28
  23.1 0.7 copy.11
  23.8 1.1 reshape.29.mixing_ref
  24.9 49.6 %all-to-all-done = f32[256,16,128]{2,1,0:T(8,128)S(1)} async-done(((f32[256,16,128]{2,1,0:T(8,128)}), f32[256,16,128]{2,1,0:T(8,128)S(1)}, u32[]{:S(2)}, u32[]{:S(2)}) %all-to-all-start) | async-done | bytes 2097184 | tf_op jit(solution)/shard_map/all_to_all | solution.py:316
  74.4 0.0 copy-done.1
  74.4 0.0 copy-done.2
  74.4 3.0 %line.1 = f32[2,2048,128]{2,1,0:T(8,128)S(1)} custom-call(f32[2,2048,128]{2,1,0:T(8,128)S(1)} %bitcast.15, bf16[128,384]{1,0:T(8,128)(2,1)S(1)} %copy-done.1, bf16[128,384]{1,0:T(8,128)(2,1)S(1)} %copy-done.2, f32[2,16,64,128]{3,2,1,0:T(8,128)S(1)} %phase.1.phases_ref, f32[64,64]{1,0:T(8,128)S(1)} %reshape.29.mixing_ref), custom_call_target="tpu_custom_call" | custom-call | tf_op jit(solution)/shard_map/line/pallas_call | solution.py:283
  77.4 0.0 copy-start
  77.4 59.6 %all_to_all.10 = f32[256,16,128]{2,1,0:T(8,128)S(1)} all-to-all(f32[256,16,128]{2,1,0:T(8,128)S(1)} %bitcast.16), channel_id=1, replica_groups=mesh['orient'=2,'slab'=128] {'orient','slab'}, dimensions={0} | all-to-all | bytes 4194304 | tf_op jit(solution)/shard_map/all_to_all | solution.py:322
  137.0 0.0 copy-done
  137.1 2.1 %close.1 = f32[2,16,128,128]{3,2,1,0:T(8,128)} custom-call(f32[2,2048,128]{2,1,0:T(8,128)S(1)} %bitcast.14, f32[128,128]{1,0:T(8,128)S(1)} %bitcast.18), custom_call_target="tpu_custom_call" | custom-call | tf_op jit(solution)/shard_map/close/pallas_call | solution.py:295
Async XLA Ops:
  5.6 15.7 %copy-start.3 = (f32[3,64]{1,0:T(4,128)S(1)}, f32[3,64]{1,0:T(4,128)}, u32[]{:S(2)}) copy-start(f32[3,64]{1,0:T(4,128)} %orientations_ref.3) | copy-start | bytes 2308
  5.6 17.0 %copy-start.4 = (f32[64]{0:T(128)S(1)}, f32[64]{0:T(128)}, u32[]{:S(2)}) copy-start(f32[64]{0:T(128)} %param.10) | copy-start | bytes 772
  5.6 68.8 %all-to-all-start = ((f32[256,16,128]{2,1,0:T(8,128)}), f32[256,16,128]{2,1,0:T(8,128)S(1)}, u32[]{:S(2)}, u32[]{:S(2)}) async-start(f32[256,16,128]{2,1,0:T(8,128)} %bitcast.19), calls=%async_computation | async-start | bytes 4194304 | tf_op jit(solution)/shard_map/all_to_all | solution.py:316
  21.2 53.2 %copy-start.1 = (bf16[128,384]{1,0:T(8,128)(2,1)S(1)}, bf16[128,384]{1,0:T(8,128)(2,1)}, u32[]{:S(2)}) copy-start(bf16[128,384]{1,0:T(8,128)(2,1)} %constant.96.clone.forward_ref) | copy-start | bytes 294916
  21.2 53.2 %copy-start.2 = (bf16[128,384]{1,0:T(8,128)(2,1)S(1)}, bf16[128,384]{1,0:T(8,128)(2,1)}, u32[]{:S(2)}) copy-start(bf16[128,384]{1,0:T(8,128)(2,1)} %constant.97.clone.inverse_ref) | copy-start | bytes 294916
  77.4 59.6 %copy-start = (f32[1,128,128]{2,1,0:T(8,128)S(1)}, f32[1,128,128]{2,1,0:T(8,128)}, u32[]{:S(2)}) copy-start(f32[1,128,128]{2,1,0:T(8,128)} %param.8) | copy-start | bytes 196612

commit v5 on v4

--- a/solution.py
+++ b/solution.py
@@ -20,7 +20,7 @@
 SMALL = pltpu.CompilerParams(vmem_limit_bytes=16 * 1024 * 1024)
 LARGE = pltpu.CompilerParams()
 BATCH = 8
-STRIPS = 2
+STRIPS = 8
 MIX_UNROLL = 32
 
 
@@ -141,9 +141,8 @@
             moved.append(narrow_product(shift_y, narrow_product(damped, shift_x)))
         first, second = moved
         low = low_lanes(first.shape)
-        rows = pl.ds(row, first.shape[0], stride=count)
-        out_ref[0, rows, :] = jnp.where(low, first, swap(second))
-        out_ref[1, rows, :] = jnp.where(low, swap(first), second)
+        out_ref[0, :, n, :] = jnp.where(low, first, swap(second))
+        out_ref[1, :, n, :] = jnp.where(low, swap(first), second)
 
 
 def line_kernel(depth, lines_ref, forward_ref, inverse_ref, phases_ref, mixing_ref, out_ref, advected_ref):
@@ -228,18 +227,26 @@
             out_ref[group, row] = jnp.where(quarters < 2, low, high)
 
 
-def close_kernel(mixed_ref, field_ref, out_ref):
-    depth = out_ref.shape[2]
-    count = out_ref.shape[1]
-    base = pl.program_id(0) * depth
-    damping = jnp.exp(-0.5 * HALF_STEP * field_ref[pl.ds(base, depth), :])
-    low = low_lanes(damping.shape)
-    for row in range(count):
-        rows = pl.ds(base * count + row, depth, stride=count)
-        first = mixed_ref[0, rows, :]
-        second = mixed_ref[1, rows, :]
-        out_ref[0, row] = jnp.where(low, first, swap(second)) * damping
-        out_ref[1, row] = jnp.where(low, swap(first), second) * damping
+def close_kernel(mixed_ref, field_ref, out_ref, held_ref, sems):
+    _, count, rows, _ = held_ref.shape
+    depth = rows // STRIPS
+    copies = []
+    for strip in range(STRIPS):
+        base = strip * depth
+        own = pl.ds(base, depth)
+        damping = jnp.exp(-0.5 * HALF_STEP * field_ref[own, :])
+        low = low_lanes(damping.shape)
+        for row in range(count):
+            taken = pl.ds(base * count + row, depth, stride=count)
+            first = mixed_ref[0, taken, :]
+            second = mixed_ref[1, taken, :]
+            held_ref[0, row, own, :] = jnp.where(low, first, swap(second)) * damping
+            held_ref[1, row, own, :] = jnp.where(low, swap(first), second) * damping
+        copy = pltpu.make_async_copy(held_ref.at[:, :, own], out_ref.at[:, :, own], sems.at[strip])
+        copy.start()
+        copies.append(copy)
+    for copy in copies:
+        copy.wait()
 
 
 def whole(shape):
@@ -248,7 +255,6 @@
 
 def run_plane(propagator, plane, orientations, start):
     _, count, rows, cols = propagator.shape
-    message = (2, rows * count, cols)
     return pl.pallas_call(
         functools.partial(plane_kernel, count, start),
         grid=(count // BATCH,),
@@ -258,8 +264,8 @@
             whole(orientations.shape),
             whole((cols, cols)),
         ],
-        out_specs=whole(message),
-        out_shape=jax.ShapeDtypeStruct(message, jnp.float32),
+        out_specs=pl.BlockSpec((2, rows, BATCH, cols), lambda row: (0, 0, row, 0)),
+        out_shape=jax.ShapeDtypeStruct((2, rows, count, cols), jnp.float32),
         scratch_shapes=[
             pltpu.VMEM((rows, cols), jnp.float32),
             pltpu.VMEM((2 * orientations.shape[1], cols), jnp.float32),
@@ -290,14 +296,13 @@
 
 
 def run_close(mixed, plane, count):
-    rows, cols = plane.shape
-    strip = rows // STRIPS
+    shape = (2, count) + plane.shape
     return pl.pallas_call(
         close_kernel,
-        grid=(rows // strip,),
         in_specs=[pl.BlockSpec(memory_space=pltpu.VMEM)] * 2,
-        out_specs=pl.BlockSpec((2, count, strip, cols), lambda step: (0, 0, step, 0)),
-        out_shape=jax.ShapeDtypeStruct((2, count, rows, cols), jnp.float32),
+        out_specs=pl.BlockSpec(memory_space=pl.ANY),
+        out_shape=jax.ShapeDtypeStruct(shape, jnp.float32),
+        scratch_shapes=[pltpu.VMEM(shape, jnp.float32), pltpu.SemaphoreType.DMA((STRIPS,))],
         compiler_params=SMALL,
         name="close",
     )(mixed, plane)
@@ -318,9 +323,10 @@
     matrix = mixing_matrix(orientations, weights)
     matrix = matrix.reshape(groups, 2, count, groups, 2, count).transpose(1, 0, 2, 4, 3, 5)
     matrix = matrix.reshape(2 * own, 2 * own)
-    back = run_line(lines.reshape(sent.shape), phases, matrix, total_z)
+    message = (groups, slabs * count, cols)
+    back = run_line(lines.reshape(message), phases, matrix, total_z)
     mixed = lax.all_to_all(back.reshape(groups * slabs, count, cols), AXES, 0, 0, tiled=True)
-    result = run_close(mixed.reshape(sent.shape), plane, count)
+    result = run_close(mixed.reshape(message), plane, count)
     return result.reshape(own, 1, rows, cols)
 
 

time: 139 us -> 139 us (level)
  no operation moved by 1% of the time
where the time goes in v5:
time: 139 us
  blocking collectives  59.6 us (43%)
  waiting for transfers between devices  49.6 us (36%)
  starting transfers between devices  15.6 us (11%)
  Pallas kernels  11.5 us (8%)
  local copies, waits for them, and re-layouts  1.95 us (1%)
    all_to_all x1, blocking collectives, local(): lax.all_to_all(back.reshape(groups * slabs, count, cols), AXES, 0, 0, til...  59.6 us
    all_to_all x1, waiting for transfers between devices, local(): lax.all_to_all(sent.reshape(groups * slabs, count, cols), AXES, 0, 0, til...  49.6 us
    all_to_all x1, starting transfers between devices, local(): lax.all_to_all(sent.reshape(groups * slabs, count, cols), AXES, 0, 0, til...  15.6 us
    pallas_call x1, Pallas kernels, run_plane(): pl.pallas_call(functools.partial(plane_kernel, count, start), grid=(count...  5.51 us
    pallas_call x1, Pallas kernels, run_line(): pl.pallas_call(functools.partial(line_kernel, total_z), out_shape=jax.Sha...  2.99 us
  transfers between devices with their start and end apart: 1, of which 1 were waited for; matrix products, arithmetic and copies ran while one was open for 2% of the time, Pallas kernels for 1%

profile of v5, /device:TPU:1, one launch (start us, length us, event | category | flops | bytes accessed | tf_op | source)
XLA Modules:
  0.0 138.6 jit_solution(1392614453378984910)
XLA Ops:
  0.0 5.5 %plane.1 = f32[2,128,16,128]{3,2,1,0:T(8,128)} custom-call(f32[2,16,128,128]{3,2,1,0:T(8,128)} %bitcast.20, f32[128,128]{1,0:T(8,128)} %bitcast.17, f32[3,64]{1,0:T(4,128)} %orientations_ref.3, f32[128,128]{1,0:T(8,128)} %constant.95.clone.inverse_ref), custom_call_target="tpu_custom_call" | custom-call | tf_op jit(solution)/shard_map/plane/pallas_call | solution.py:258
  5.5 0.0 copy-start.3
  5.5 0.0 copy-start.4
  5.5 15.6 %all-to-all-start = ((f32[256,16,128]{2,1,0:T(8,128)}), f32[256,16,128]{2,1,0:T(8,128)S(1)}, u32[]{:S(2)}, u32[]{:S(2)}) async-start(f32[256,16,128]{2,1,0:T(8,128)} %bitcast.19), calls=%async_computation | async-start | bytes 4194304 | tf_op jit(solution)/shard_map/all_to_all | solution.py:321
  21.2 0.0 copy-done.3
  21.2 0.0 copy-start.1
  21.2 0.0 copy-start.2
  21.2 1.3 phase.1.phases_ref
  22.6 0.0 copy-done.4
  22.6 0.3 add_multiply_fusion
  22.9 0.2 reshape.28
  23.0 0.7 copy.11
  23.8 1.1 reshape.29.mixing_ref
  24.8 49.6 %all-to-all-done = f32[256,16,128]{2,1,0:T(8,128)S(1)} async-done(((f32[256,16,128]{2,1,0:T(8,128)}), f32[256,16,128]{2,1,0:T(8,128)S(1)}, u32[]{:S(2)}, u32[]{:S(2)}) %all-to-all-start) | async-done | bytes 2097184 | tf_op jit(solution)/shard_map/all_to_all | solution.py:321
  74.4 0.0 copy-done.1
  74.4 0.0 copy-done.2
  74.4 3.0 %line.1 = f32[2,2048,128]{2,1,0:T(8,128)S(1)} custom-call(f32[2,2048,128]{2,1,0:T(8,128)S(1)} %bitcast.15, bf16[128,384]{1,0:T(8,128)(2,1)S(1)} %copy-done.1, bf16[128,384]{1,0:T(8,128)(2,1)S(1)} %copy-done.2, f32[2,16,64,128]{3,2,1,0:T(8,128)S(1)} %phase.1.phases_ref, f32[64,64]{1,0:T(8,128)S(1)} %reshape.29.mixing_ref), custom_call_target="tpu_custom_call" | custom-call | tf_op jit(solution)/shard_map/line/pallas_call | solution.py:289
  77.4 0.0 copy-start
  77.4 59.6 %all_to_all.10 = f32[256,16,128]{2,1,0:T(8,128)S(1)} all-to-all(f32[256,16,128]{2,1,0:T(8,128)S(1)} %bitcast.16), channel_id=1, replica_groups=mesh['orient'=2,'slab'=128] {'orient','slab'}, dimensions={0} | all-to-all | bytes 4194304 | tf_op jit(solution)/shard_map/all_to_all | solution.py:328
  137.0 0.0 copy-done
  137.0 1.6 %close.1 = f32[2,16,128,128]{3,2,1,0:T(8,128)} custom-call(f32[2,2048,128]{2,1,0:T(8,128)S(1)} %bitcast.14, f32[128,128]{1,0:T(8,128)S(1)} %bitcast.18), custom_call_target="tpu_custom_call" | custom-call | tf_op jit(solution)/shard_map/close/pallas_call | solution.py:300
Async XLA Ops:
  5.5 15.7 %copy-start.3 = (f32[3,64]{1,0:T(4,128)S(1)}, f32[3,64]{1,0:T(4,128)}, u32[]{:S(2)}) copy-start(f32[3,64]{1,0:T(4,128)} %orientations_ref.3) | copy-start | bytes 2308
  5.5 17.0 %copy-start.4 = (f32[64]{0:T(128)S(1)}, f32[64]{0:T(128)}, u32[]{:S(2)}) copy-start(f32[64]{0:T(128)} %param.10) | copy-start | bytes 772
  5.5 68.8 %all-to-all-start = ((f32[256,16,128]{2,1,0:T(8,128)}), f32[256,16,128]{2,1,0:T(8,128)S(1)}, u32[]{:S(2)}, u32[]{:S(2)}) async-start(f32[256,16,128]{2,1,0:T(8,128)} %bitcast.19), calls=%async_computation | async-start | bytes 4194304 | tf_op jit(solution)/shard_map/all_to_all | solution.py:321
  21.2 53.2 %copy-start.1 = (bf16[128,384]{1,0:T(8,128)(2,1)S(1)}, bf16[128,384]{1,0:T(8,128)(2,1)}, u32[]{:S(2)}) copy-start(bf16[128,384]{1,0:T(8,128)(2,1)} %constant.96.clone.forward_ref) | copy-start | bytes 294916
  21.2 53.2 %copy-start.2 = (bf16[128,384]{1,0:T(8,128)(2,1)S(1)}, bf16[128,384]{1,0:T(8,128)(2,1)}, u32[]{:S(2)}) copy-start(bf16[128,384]{1,0:T(8,128)(2,1)} %constant.97.clone.inverse_ref) | copy-start | bytes 294916
  77.4 59.6 %copy-start = (f32[1,128,128]{2,1,0:T(8,128)S(1)}, f32[1,128,128]{2,1,0:T(8,128)}, u32[]{:S(2)}) copy-start(f32[1,128,128]{2,1,0:T(8,128)} %param.8) | copy-start | bytes 196612
